TPU v7x, 32 devices: a whole 2x2x4 slice. The times are simulated.
32 devices in a mesh: seq: 8 (over y, x, core), tp: 4 (over z).
Axes of the slice: x: 2, y: 2, z: 4, core: 2. Of those that a mesh axis runs over, the one named last changes fastest.
Arguments:
- byte_states: bfloat16 [2048, 1024], P('seq'), may hold values from -6 to 6
- enc_gain: bfloat16 [1024], replicated, may hold values from 0.25 to 1.75
- enc_qkv: bfloat16 [3, 1024, 1024], P(None, None, 'tp')
- enc_proj_out: bfloat16 [1024, 1024], P('tp'), may hold values from -0.1875 to 0.1875
- starts: int32 [8, 64], P('seq'), may hold values from 0 to 2048, as said below
- counts: int32 [8], P('seq'), may hold values from 32 to 64, as said below
- lift: bfloat16 [1024, 4096], P(None, 'tp')
- cross_kv: bfloat16 [2, 1024, 4096], P(None, None, 'tp')
- latent_gain: bfloat16 [4096], replicated, may hold values from 0.25 to 1.75
- lat_qkv: bfloat16 [3, 4096, 2048], P(None, 'seq', 'tp')
- lat_proj_out: bfloat16 [2048, 4096], P('tp', 'seq'), may hold values from -0.75 to 0.75
Outputs:
- byte_out: bfloat16 [2048, 1024], P('seq')
- latent_out: bfloat16 [512, 4096], P('seq', 'tp')
Inputs may be any that keep to these rules, and one draw needn't show every extreme that they name: `starts`: row s lists in increasing order the first byte (counted over all 2048 bytes) of each patch beginning in bytes s * 256 to (s + 1) * 256 - 1, then 2048 in unused places. Byte 0 begins a patch; every row's first patch begins fewer than 8 bytes into its block, and in some row exactly 7 bytes in. counts[s] is the number of patches listed in row s of starts; some row holds 64.
All inputs are finite; a program needn't handle non-finite values.
Results may differ from a plain program's by a relative error of at most 0.018.
Values may be sent and summed in bfloat16 or wider, within the bound.
A program may use at most 128 MiB of HBM per device.

v0:
```python
import math

import jax
import jax.numpy as jnp
from jax import lax
from jax.sharding import PartitionSpec as P

EH = 64
HD = 128
WIN = 512
SPILL = 8


epsilon = 1e-05
rope_base = 500000.0
far_position = 1 << 30


def from_behind(value, axis, steps):
    count = lax.axis_size(axis)
    leading, last = (max(0, -steps), min(count, count - steps))
    return lax.ppermute(value, axis, [(source, source + steps) for source in range(leading, last)])


def prefix(value, axis, join, neutral):
    count, mine = (lax.axis_size(axis), lax.axis_index(axis))
    pieces = lax.all_gather(value, axis)
    subtotal = jnp.full_like(value, 0) + jnp.asarray(neutral, value.dtype)

    def hop(position, subtotal):
        longer = join(subtotal, pieces[position])
        return jnp.where(position < mine, longer, subtotal)

    return lax.fori_loop(0, count - 1, hop, subtotal)


def shortened(value):

    def short(part):
        return part.astype(jnp.bfloat16) if part.dtype == jnp.float32 else part

    return jax.tree.map(short, value)


def rms_scale(values, gain_row):
    mean_square = jnp.mean(values * values, axis=-1, keepdims=True)
    return values * lax.rsqrt(mean_square + epsilon) * gain_row


def masked_softmax(scores, allowed):
    scores = jnp.where(allowed, scores, -1e30)
    largest = jnp.max(scores, axis=-1, keepdims=True)
    raised = jnp.where(allowed, jnp.exp(scores - largest), 0.0)
    return raised / jnp.sum(raised, axis=-1, keepdims=True)


def rotate(values, position):
    halfway = values.shape[-1] // 2
    frequency = jnp.power(
        rope_base, -2.0 * jnp.arange(halfway, dtype=jnp.float32) / values.shape[-1]
    )
    angles = position.astype(jnp.float32)[:, None] * frequency[None, :]
    cosine = jnp.cos(angles)[:, None, :]
    sine_rows = jnp.sin(angles)[:, None, :]
    lower_half = values[..., :halfway]
    upper_half = values[..., halfway:]
    return jnp.concatenate(
        [
            lower_half * cosine - upper_half * sine_rows,
            upper_half * cosine + lower_half * sine_rows,
        ],
        axis=-1,
    )


def patch_block(extended, first_byte, end_byte, in_use, anchor, lift, cross_kv):
    columns = anchor + jnp.arange(extended.shape[0], dtype=jnp.int32)
    inside = (
        (columns[None, :] >= first_byte[:, None])
        & (columns[None, :] < end_byte[:, None])
        & in_use[:, None]
    )
    member = inside.astype(jnp.bfloat16)
    totals = jnp.dot(member, extended, preferred_element_type=jnp.float32)
    lengths = jnp.maximum(jnp.sum(inside.astype(jnp.float32), axis=1), 1.0)
    pooled = (totals / lengths[:, None]).astype(jnp.bfloat16)
    lifted = jnp.dot(pooled, lift, preferred_element_type=jnp.float32)
    key_rows = jnp.dot(extended, cross_kv[0], preferred_element_type=jnp.float32).astype(
        jnp.bfloat16
    )
    value_rows = jnp.dot(extended, cross_kv[1], preferred_element_type=jnp.float32).astype(
        jnp.bfloat16
    )
    slot_total = first_byte.shape[0]
    head_count = lifted.shape[1] // HD
    queries = lifted.astype(jnp.bfloat16).reshape(slot_total, head_count, HD)
    scores = jnp.einsum(
        "phd,khd->hpk",
        queries,
        key_rows.reshape(-1, head_count, HD),
        preferred_element_type=jnp.float32,
    ) * (1.0 / math.sqrt(HD))
    allowed = inside | (~in_use)[:, None] & (columns[None, :] == anchor)
    weights = masked_softmax(scores, allowed[None]).astype(jnp.bfloat16)
    crossed = jnp.einsum(
        "hpk,khd->phd",
        weights,
        value_rows.reshape(-1, head_count, HD),
        preferred_element_type=jnp.float32,
    )
    crossed = crossed.reshape(slot_total, head_count * HD)
    return jnp.where(in_use[:, None], lifted + crossed, 0.0).astype(jnp.bfloat16)


def add_counts(earlier, later):
    return earlier + later


def shards(
    byte_states,
    enc_gain,
    enc_qkv,
    enc_proj_out,
    starts,
    counts,
    lift,
    cross_kv,
    latent_gain,
    lat_qkv,
    lat_proj_out,
):
    byte_rows = byte_states.shape[0]
    anchor = lax.axis_index("seq") * byte_rows
    states = byte_states.astype(jnp.float32)
    normed = rms_scale(states, enc_gain.astype(jnp.float32)).astype(jnp.bfloat16)
    projected = jnp.einsum(
        "bd,idc->ibc", normed, enc_qkv, preferred_element_type=jnp.float32
    ).astype(jnp.bfloat16)
    reach_blocks = max(WIN // byte_rows, 1)
    tail_rows = min(WIN, byte_rows)
    key_parts = []
    value_parts = []
    for distance in range(reach_blocks, 0, -1):
        moved_keys, moved_values = from_behind(
            (projected[1, byte_rows - tail_rows :], projected[2, byte_rows - tail_rows :]),
            "seq",
            distance,
        )
        key_parts.append(moved_keys)
        value_parts.append(moved_values)
    key_rows = jnp.concatenate(key_parts + [projected[1]], axis=0)
    value_rows = jnp.concatenate(value_parts + [projected[2]], axis=0)
    head_count = projected.shape[2] // EH
    scores = jnp.einsum(
        "qhd,khd->hqk",
        projected[0].reshape(byte_rows, head_count, EH),
        key_rows.reshape(-1, head_count, EH),
        preferred_element_type=jnp.float32,
    ) * (1.0 / math.sqrt(EH))
    query_pos = anchor + jnp.arange(byte_rows, dtype=jnp.int32)
    key_pos = anchor - WIN + jnp.arange(WIN + byte_rows, dtype=jnp.int32)
    allowed = (
        (key_pos[None, :] <= query_pos[:, None])
        & (key_pos[None, :] > query_pos[:, None] - WIN)
        & (key_pos[None, :] >= 0)
    )
    weights = masked_softmax(scores, allowed[None]).astype(jnp.bfloat16)
    attended = jnp.einsum(
        "hqk,khd->qhd",
        weights,
        value_rows.reshape(-1, head_count, EH),
        preferred_element_type=jnp.float32,
    )
    attended = attended.reshape(byte_rows, head_count * EH).astype(jnp.bfloat16)
    blended = lax.psum(jnp.dot(attended, enc_proj_out, preferred_element_type=jnp.float32), "tp")
    encoded = (states + blended).astype(jnp.bfloat16)
    patch_count = counts[0]
    local_starts = starts[0]
    first_local = (local_starts[0:1] - anchor).astype(jnp.bfloat16)
    next_rows, next_first = from_behind((encoded[:SPILL], first_local), "seq", -1)
    next_first = next_first.astype(jnp.int32)[0]
    extended = jnp.concatenate([encoded, next_rows], axis=0)
    slot_ids = jnp.arange(local_starts.shape[0], dtype=jnp.int32)
    in_use = slot_ids < patch_count
    following = jnp.concatenate([local_starts[1:], jnp.zeros((1,), jnp.int32)])
    patch_end = jnp.where(slot_ids + 1 < patch_count, following, anchor + byte_rows + next_first)
    patches = patch_block(extended, local_starts, patch_end, in_use, anchor, lift, cross_kv)
    offset = prefix(counts, "seq", add_counts, jnp.zeros((1,), jnp.int32))[0]
    position = offset + slot_ids
    slot_total = patches.shape[0]
    full_rows = lax.all_gather(patches, "tp", axis=1, tiled=True)
    normed_rows = rms_scale(full_rows.astype(jnp.float32), latent_gain.astype(jnp.float32)).astype(
        jnp.bfloat16
    )
    inner_width = lat_qkv.shape[2]
    projected = jnp.einsum(
        "pd,idc->ipc",
        normed_rows,
        lax.all_gather(lat_qkv, "seq", axis=1, tiled=True),
        preferred_element_type=jnp.float32,
    )
    heads_here = inner_width // HD
    queries = rotate(projected[0].reshape(slot_total, heads_here, HD), position).astype(
        jnp.bfloat16
    )
    latent_keys = (
        rotate(projected[1].reshape(slot_total, heads_here, HD), position)
        .astype(jnp.bfloat16)
        .reshape(slot_total, inner_width)
    )
    latent_values = projected[2].astype(jnp.bfloat16)
    latent_pos = jnp.where(in_use, position, far_position)
    largest = jnp.full((heads_here, slot_total), -1e30, jnp.float32)
    piece_keys = lax.all_gather(latent_keys, "seq", axis=0, tiled=True)
    piece_values = lax.all_gather(latent_values, "seq", axis=0, tiled=True)
    piece_pos = lax.all_gather(shortened(latent_pos), "seq", axis=0, tiled=True)
    rows_here = piece_keys.shape[0]
    piece_scores = jnp.einsum(
        "qhd,khd->hqk",
        queries,
        piece_keys.reshape(rows_here, heads_here, HD),
        preferred_element_type=jnp.float32,
    ) * (1.0 / math.sqrt(HD))
    permitted = (piece_pos[None, :] <= position[:, None])[None]
    piece_scores = jnp.where(permitted, piece_scores, -1e30)
    renewed = jnp.maximum(largest, jnp.max(piece_scores, axis=-1))
    raised = jnp.where(permitted, jnp.exp(piece_scores - renewed[..., None]), 0.0)
    weight_sum = jnp.sum(raised, axis=-1)
    weighted = jnp.einsum(
        "hqk,khd->hqd",
        raised.astype(jnp.bfloat16),
        piece_values.reshape(rows_here, heads_here, HD),
        preferred_element_type=jnp.float32,
    )
    largest, weight_sum, weighted = (renewed, weight_sum, weighted)
    latent_heads = (
        (weighted / weight_sum[..., None])
        .transpose(1, 0, 2)
        .reshape(slot_total, inner_width)
        .astype(jnp.bfloat16)
    )
    partials = jnp.dot(
        latent_heads,
        lax.all_gather(lat_proj_out, "seq", axis=1, tiled=True),
        preferred_element_type=jnp.float32,
    )
    reduced = lax.psum_scatter(partials, "tp", scatter_dimension=1, tiled=True)
    latent = jnp.where(in_use[:, None], patches.astype(jnp.float32) + reduced, 0.0).astype(
        jnp.bfloat16
    )
    return (encoded, latent)


def solution(mesh):
    return jax.shard_map(
        shards,
        mesh=mesh,
        in_specs=(
            P("seq", None),
            P(),
            P(None, None, "tp"),
            P("tp", None),
            P("seq", None),
            P("seq"),
            P(None, "tp"),
            P(None, None, "tp"),
            P(),
            P(None, "seq", "tp"),
            P("tp", "seq"),
        ),
        out_specs=(P("seq", None), P("seq", "tp")),
        check_vma=False,
    )
```

profile of v0, /device:TPU:6, one launch (start us, length us, event | category | flops | bytes accessed | tf_op | source)
XLA Modules:
  0.0 186.8 jit_solution(6038080020906645445)
XLA Ops:
  8.1 0.8 convert_element_type.99
  8.9 1.2 fusion.40
  10.1 2.4 %fusion.30 = bf16[3,256,256]{1,2,0:T(8,128)(2,1)S(1)} fusion(bf16[3,1024,256]{2,1,0:T(8,128)(2,1)} %param.15, bf16[256,1024]{1,0:T(8,128)(2,1)} %param.13, f32[1024]{0:T(1024)S(1)} %convert_element_type.99, f32[256]{0:T(256)S(1)} %add_rsqrt_fusion), kind=kOutput, calls=%fused_computation.34 | convolution fusion | flops 403898368 | bytes 2495488 | tf_op jit(solution)/shard_map/bd,idc->ibc/dot_general | solution.py:136
  12.5 1.3 collective-permute-start.2
  13.8 1.9 %collective-permute-start.3 = (bf16[256,256]{0,1:T(8,128)(2,1)S(1)}, bf16[256,256]{0,1:T(8,128)(2,1)S(1)}, u32[]{:S(2)}, u32[]{:S(2)}) collective-permute-start(bf16[256,256]{0,1:T(8,128)(2,1)S(1)} %get-tuple-element.93), channel_id=1, source_target_pairs={{0,4},{4,8},{8,12},{12,16},{16,20},{20,24},{24,28},{1,5},{5,9},{9,... | collective-permute-start | bytes 393224 | tf_op jit(solution)/shard_map/ppermute | solution.py:22
  15.8 1.3 collective-permute-start
  17.1 1.9 %collective-permute-start.1 = (bf16[256,256]{0,1:T(8,128)(2,1)S(1)}, bf16[256,256]{0,1:T(8,128)(2,1)S(1)}, u32[]{:S(2)}, u32[]{:S(2)}) collective-permute-start(bf16[256,256]{0,1:T(8,128)(2,1)S(1)} %get-tuple-element.92), channel_id=1, source_target_pairs={{0,4},{4,8},{8,12},{12,16},{16,20},{20,24},{24,28},{1,5},{5,9},{9,... | collective-permute-start | bytes 393224 | tf_op jit(solution)/shard_map/ppermute | solution.py:22
  19.3 1.2 collective-permute-done.2
  20.6 0.5 collective-permute-done.3
  21.1 0.6 fusion.64
  21.7 1.8 fusion.112
  23.5 1.1 collective-permute-done
  24.7 0.6 collective-permute-done.1
  25.3 0.7 fusion.32
  26.3 1.4 fusion.119
  27.8 0.5 all-gather.5.cloned.1.call-update
  28.4 4.0 %collective-permute-start.4 = (bf16[1]{0:T(256)(128)(2,1)}, bf16[1]{0:T(256)(128)(2,1)}, u32[]{:S(2)}, u32[]{:S(2)}) collective-permute-start(bf16[1]{0:T(256)(128)(2,1)} %convert_element_type.108), channel_id=1, source_target_pairs={{4,0},{8,4},{12,8},{16,12},{20,16},{24,20},{28,24},{5,1},{9,5},{13... | collective-permute-start | bytes 14 | tf_op jit(solution)/shard_map/ppermute | solution.py:22
  33.2 0.6 dynamic-slice
  33.8 0.7 dynamic-update-slice
  34.5 8.0 %all-reduce = s32[8]{0:T(128)S(1)} all-reduce(s32[8]{0:T(128)S(1)} %dynamic-update-slice), channel_id=2, replica_groups=mesh['seq'=8,'tp'=4] {'seq'}, use_global_device_ids=true, to_apply=%add | all-reduce | flops 8 | bytes 64
  42.5 8.7 %while.13 = (s32[]{:T(128)}, s32[1]{0:T(128)}, s32[]{:T(128)}, s32[8,1]{0,1:T(1,128)S(1)}, s32[]{:T(128)}) while((s32[]{:T(128)}, s32[1]{0:T(128)}, s32[]{:T(128)}, s32[8,1]{0,1:T(1,128)S(1)}, s32[]{:T(128)}) %tuple.59), condition=%wide.region_8.9_spmd, body=%wide.region_7.8_spmd.sunk | while | flops 5 | bytes 107 | solution.py:34
  42.5 0.6 constant_dynamic-slice_fusion.2
  43.7 0.6 constant_dynamic-slice_fusion.2
  45.0 0.6 constant_dynamic-slice_fusion.2
  46.2 0.6 constant_dynamic-slice_fusion.2
  47.5 0.6 constant_dynamic-slice_fusion.2
  48.7 0.6 constant_dynamic-slice_fusion.2
  50.0 0.6 constant_dynamic-slice_fusion.2
  51.9 7.7 %all-reduce.1 = s32[512]{0:T(512)S(1)} all-reduce(s32[512]{0:T(512)S(1)} %select_dynamic-update-slice_fusion), channel_id=1, replica_groups=mesh['seq'=8,'tp'=4] {'seq'}, use_global_device_ids=true, to_apply=%add.1 | all-reduce | flops 512 | bytes 4096
  61.0 21.6 %all-reduce.4.cloned.1.call-done = f32[256,1024]{1,0:T(8,128)} async-done(((f32[256,1024]{1,0:T(8,128)}), f32[256,1024]{1,0:T(8,128)}) %all-reduce.4.cloned.1.call-update) | async-done | bytes 1048592 | tf_op jit(solution)/shard_map/psum | solution.py:175
  82.6 1.4 fusion.43
  84.0 2.0 %collective-permute-start.5 = (bf16[8,1024]{1,0:T(8,128)(2,1)S(1)}, bf16[8,1024]{1,0:T(8,128)(2,1)S(1)}, u32[]{:S(2)}, u32[]{:S(2)}) collective-permute-start(bf16[8,1024]{1,0:T(8,128)(2,1)S(1)} %slice.73), channel_id=1, source_target_pairs={{4,0},{8,4},{12,8},{16,12},{20,16},{24,20},{28,24},{5,1},{9,5},{13... | collective-permute-start | bytes 49160 | tf_op jit(solution)/shard_map/ppermute | solution.py:22
  86.0 1.7 collective-permute-done.5
  87.7 3.1 %fusion.23 = bf16[33,8,8,128]{3,2,1,0:T(8,128)(2,1)} fusion(bf16[2,1024,1024]{2,1,0:T(8,128)(2,1)} %param.20, bf16[8,1024]{1,0:T(8,128)(2,1)S(1)} %collective-permute-done.5, bf16[256,1024]{1,0:T(8,128)(2,1)S(1)} %fusion.43), kind=kOutput, calls=%fused_computation.30 | convolution fusion | flops 554999808 | bytes 3178496 | tf_op jit(solution)/shard_map/dot_general | solution.py:88
  90.8 0.7 fusion.33
  91.5 2.4 %fusion.113 = (f32[8,64]{1,0:T(8,128)S(1)}, f32[8,64,264]{2,1,0:T(8,128)}) fusion(bf16[33,8,8,128]{3,2,1,0:T(8,128)(2,1)} %fusion.23, pred[64,264]{1,0:T(8,128)(4,1)S(1)} %and_or_fusion, f32[64,1024]{1,0:T(8,128)S(1)} %fusion.33), kind=kOutput, calls=%fused_computation.147 | convolution fusion | flops 35344648 | bytes 1362432 | tf_op jit(solution)/shard_map/sub | solution.py:53
  93.9 2.6 %fusion.26 = bf16[33,8,8,128]{3,2,1,0:T(8,128)(2,1)S(1)} fusion(bf16[2,1024,1024]{2,1,0:T(8,128)(2,1)} %param.20, bf16[8,1024]{1,0:T(8,128)(2,1)S(1)} %collective-permute-done.5, bf16[256,1024]{1,0:T(8,128)(2,1)S(1)} %fusion.43), kind=kOutput, calls=%fused_computation.31 | convolution fusion | flops 554999808 | bytes 3178496 | tf_op jit(solution)/shard_map/dot_general | solution.py:91
  96.5 0.3 convolution_bitcast_fusion.1
  96.9 15.5 %all_gather.27 = bf16[64,4096]{1,0:T(8,128)(2,1)S(1)} all-gather(bf16[64,1024]{1,0:T(8,128)(2,1)S(1)} %fusion.73), channel_id=1, replica_groups=mesh['seq'=8,'tp'=4] {'tp'}, dimensions={1}, use_global_device_ids=true | all-gather | bytes 655360 | tf_op jit(solution)/shard_map/all_gather | solution.py:191
  112.6 7.5 %convolution_bitcast_fusion = f32[3,64,512]{2,1,0:T(8,128)S(1)} fusion(bf16[3,4096,512]{2,1,0:T(8,128)(2,1)} %all-gather.5.cloned.1.call-done, bf16[64,4096]{1,0:T(8,128)(2,1)S(1)} %all_gather.27, f32[4096]{0:T(1024)S(1)} %convert_element_type.118, f32[64]{0:T(128)S(1)} %add_rsqrt_fusion.1), kind=kOutput, calls=%fused_computation.35 | convolution fusion | flops 806354944 | bytes 13517056 | tf_op jit(solution)/shard_map/pd,idc->ipc/dot_general | solution.py:196
  120.7 10.3 %all_gather.29 = bf16[512,512]{1,0:T(8,128)(2,1)S(1)} all-gather(bf16[64,512]{1,0:T(8,128)(2,1)S(1)} %copy_bitcast_fusion), channel_id=1, replica_groups=mesh['seq'=8,'tp'=4] {'seq'}, dimensions={0}, use_global_device_ids=true | all-gather | bytes 589824 | tf_op jit(solution)/shard_map/all_gather | solution.py:214
  131.3 11.9 %all-gather.1 = bf16[1,512,512]{2,1,0:T(8,128)(2,1)S(1)} all-gather(bf16[1,64,512]{2,1,0:T(8,128)(2,1)S(1)} %slice.101), channel_id=3, replica_groups=mesh['seq'=8,'tp'=4] {'seq'}, dimensions={1}, use_global_device_ids=true | all-gather | bytes 589824 | tf_op jit(solution)/shard_map/all_gather | solution.py:215
  143.1 0.9 reshape.384
  144.1 0.4 fusion.118
  144.7 1.3 fusion.36
  146.0 4.0 %fusion.80 = f32[64,4096]{1,0:T(8,128)} fusion(bf16[512,4096]{1,0:T(8,128)(2,1)} %all-gather.7.cloned.1.call-done, bf16[4,8,8,128]{3,2,1,0:T(8,128)(2,1)S(1)} %fusion.36), kind=kOutput, calls=%fused_computation.100 | convolution fusion | flops 268435456 | bytes 5308416 | tf_op jit(solution)/shard_map/dot_general | solution.py:242
  150.1 27.6 %reduce-scatter.2.cloned.1.call-done = f32[64,1024]{1,0:T(8,128)} async-done(((f32[64,4096]{1,0:T(8,128)}), f32[64,1024]{1,0:T(8,128)}) %reduce-scatter.2.cloned.1.call-update) | async-done | bytes 262160 | tf_op jit(solution)/shard_map/reduce_scatter | solution.py:247
  177.7 1.7 select_convert_fusion
  (65 shorter events, 3.1 us)
Async XLA Ops:
  8.0 82.8 %copy-start = (bf16[1024,1024]{1,0:T(8,128)(2,1)S(1)}, bf16[1024,1024]{1,0:T(8,128)(2,1)}, u32[]{:S(2)}) copy-start(bf16[1024,1024]{1,0:T(8,128)(2,1)} %param.19) | copy-start | bytes 6291460
  8.0 74.6 %all-reduce.4.cloned.1.call-start = ((), (), s32[]{:S(2)}) async-start(), calls=%async_computation.1 | async-start | bytes 2097152 | tf_op jit(solution)/shard_map/psum | solution.py:175
  12.5 8.0 %collective-permute-start.2 = (bf16[256,256]{0,1:T(8,128)(2,1)S(1)}, bf16[256,256]{0,1:T(8,128)(2,1)S(1)}, u32[]{:S(2)}, u32[]{:S(2)}) collective-permute-start(bf16[256,256]{0,1:T(8,128)(2,1)S(1)} %get-tuple-element.93), channel_id=1, source_target_pairs={{0,8},{4,12},{8,16},{12,20},{16,24},{20,28},{1,9},{5,13},{9,17},{1... | collective-permute-start | bytes 393224 | tf_op jit(solution)/shard_map/ppermute | solution.py:22
  13.8 7.2 %collective-permute-start.3 = (bf16[256,256]{0,1:T(8,128)(2,1)S(1)}, bf16[256,256]{0,1:T(8,128)(2,1)S(1)}, u32[]{:S(2)}, u32[]{:S(2)}) collective-permute-start(bf16[256,256]{0,1:T(8,128)(2,1)S(1)} %get-tuple-element.93), channel_id=1, source_target_pairs={{0,4},{4,8},{8,12},{12,16},{16,20},{20,24},{24,28},{1,5},{5,9},{9,... | collective-permute-start | bytes 393224 | tf_op jit(solution)/shard_map/ppermute | solution.py:22
  15.8 8.9 %collective-permute-start = (bf16[256,256]{0,1:T(8,128)(2,1)S(1)}, bf16[256,256]{0,1:T(8,128)(2,1)S(1)}, u32[]{:S(2)}, u32[]{:S(2)}) collective-permute-start(bf16[256,256]{0,1:T(8,128)(2,1)S(1)} %get-tuple-element.92), channel_id=1, source_target_pairs={{0,8},{4,12},{8,16},{12,20},{16,24},{20,28},{1,9},{5,13},{9,17},{1... | collective-permute-start | bytes 393224 | tf_op jit(solution)/shard_map/ppermute | solution.py:22
  17.1 8.2 %collective-permute-start.1 = (bf16[256,256]{0,1:T(8,128)(2,1)S(1)}, bf16[256,256]{0,1:T(8,128)(2,1)S(1)}, u32[]{:S(2)}, u32[]{:S(2)}) collective-permute-start(bf16[256,256]{0,1:T(8,128)(2,1)S(1)} %get-tuple-element.92), channel_id=1, source_target_pairs={{0,4},{4,8},{8,12},{12,16},{16,20},{20,24},{24,28},{1,5},{5,9},{9,... | collective-permute-start | bytes 393224 | tf_op jit(solution)/shard_map/ppermute | solution.py:22
  25.3 1.0 copy-start.3
  26.0 2.4 %copy-start.5 = (s32[1,64]{1,0:T(1,128)S(1)}, s32[1,64]{1,0:T(1,128)}, u32[]{:S(2)}) copy-start(s32[1,64]{1,0:T(1,128)} %param.17) | copy-start | bytes 772
  26.0 7.2 %copy-start.6 = (u32[32]{0:T(128)S(1)}, u32[32]{0:T(128)}, u32[]{:S(2)}) copy-start(u32[32]{0:T(128)} %constant.80) | copy-start | bytes 388
  26.0 25.9 %copy-start.4 = (bf16[4096]{0:T(1024)(128)(2,1)S(1)}, bf16[4096]{0:T(1024)(128)(2,1)}, u32[]{:S(2)}) copy-start(bf16[4096]{0:T(1024)(128)(2,1)} %param.21) | copy-start | bytes 24580
  26.0 56.6 %copy-start.1 = (bf16[256,1024]{1,0:T(8,128)(2,1)S(1)}, bf16[256,1024]{1,0:T(8,128)(2,1)}, u32[]{:S(2)}) copy-start(bf16[256,1024]{1,0:T(8,128)(2,1)} %param.13) | copy-start | bytes 1572868
  27.7 84.9 %all-gather.5.cloned.1.call-start = ((), (), s32[]{:S(2)}) async-start(), calls=%async_computation.2 | async-start | bytes 14155776 | tf_op jit(solution)/shard_map/all_gather | solution.py:199
  28.3 117.7 %all-gather.7.cloned.1.call-start = ((), (), s32[]{:S(2)}) async-start(), calls=%async_computation.3 | async-start | bytes 4718592 | tf_op jit(solution)/shard_map/all_gather | solution.py:244
  28.4 31.6 %collective-permute-start.4 = (bf16[1]{0:T(256)(128)(2,1)}, bf16[1]{0:T(256)(128)(2,1)}, u32[]{:S(2)}, u32[]{:S(2)}) collective-permute-start(bf16[1]{0:T(256)(128)(2,1)} %convert_element_type.108), channel_id=1, source_target_pairs={{4,0},{8,4},{12,8},{16,12},{20,16},{24,20},{28,24},{5,1},{9,5},{13... | collective-permute-start | bytes 14 | tf_op jit(solution)/shard_map/ppermute | solution.py:22
  32.5 145.2 %reduce-scatter.2.cloned.1.call-start = ((), (), s32[]{:S(2)}) async-start(), calls=%async_computation.4 | async-start | bytes 1310720 | tf_op jit(solution)/shard_map/reduce_scatter | solution.py:247
  84.0 9.9 %copy-start.2 = (bf16[256,1024]{1,0:T(8,128)(2,1)}, bf16[256,1024]{1,0:T(8,128)(2,1)S(1)}, u32[]{:S(2)}) copy-start(bf16[256,1024]{1,0:T(8,128)(2,1)S(1)} %fusion.43) | copy-start | bytes 1572868
  84.0 3.7 %collective-permute-start.5 = (bf16[8,1024]{1,0:T(8,128)(2,1)S(1)}, bf16[8,1024]{1,0:T(8,128)(2,1)S(1)}, u32[]{:S(2)}, u32[]{:S(2)}) collective-permute-start(bf16[8,1024]{1,0:T(8,128)(2,1)S(1)} %slice.73), channel_id=1, source_target_pairs={{4,0},{8,4},{12,8},{16,12},{20,16},{24,20},{28,24},{5,1},{9,5},{13... | collective-permute-start | bytes 49160 | tf_op jit(solution)/shard_map/ppermute | solution.py:22
  93.9 2.6 %copy-start.7 = (f32[8,64,264]{2,1,0:T(8,128)S(1)}, f32[8,64,264]{2,1,0:T(8,128)}, u32[]{:S(2)}) copy-start(f32[8,64,264]{2,1,0:T(8,128)} %get-tuple-element.112) | copy-start | bytes 1622020
Sparse Core Ops, SparseCore 0:
  27.8 54.7 all-reduce.3
  150.2 27.4 reduce-scatter.1
Sparse Core Ops, SparseCore 1:
  30.1 73.8 all-gather.4
  105.8 39.8 all-gather.6
where the time goes:
time: 189 us; the launch traced here: 187 us
  waiting for transfers between devices  55 us (29%)
  blocking collectives  53.3 us (28%)
  matrix products  27.3 us (14%)
  between operations  17.8 us (9%)
  starting transfers between devices  12.6 us (7%)
  other arithmetic  8.74 us (5%)
  local copies, waits for them, and re-layouts  7.48 us (4%)
  loops' own time  4.55 us (2%)
    reduce_scatter x1, waiting for transfers between devices, shards(): reduced = lax.psum_scatter(partials, 'tp', scatter_dimension=1, tiled=True)  27.6 us
    psum x1, waiting for transfers between devices, shards(): lax.psum(jnp.dot(attended, enc_proj_out, preferred_element_type=jnp.float...  21.6 us
    unnamed x2, blocking collectives  15.6 us
    all_gather x1, blocking collectives, shards(): full_rows = lax.all_gather(patches, 'tp', axis=1, tiled=True)  15.5 us
    ppermute x6, starting transfers between devices, from_behind(): lax.ppermute(value, axis, [(source, source + steps) for source in range(l...  12.4 us
    all_gather x1, blocking collectives, shards(): piece_values = lax.all_gather(latent_values, 'seq', axis=0, tiled=True)  11.9 us
    all_gather x1, blocking collectives, shards(): piece_keys = lax.all_gather(latent_keys, 'seq', axis=0, tiled=True)  10.3 us
    dot_general x1, matrix products, shards(): jnp.einsum('pd,idc->ipc', normed_rows, lax.all_gather(lat_qkv, 'seq', axi...  7.47 us
  transfers between devices with their start and end apart: 10, of which 7 were waited for; matrix products, arithmetic and copies ran while one was open for 17% of the time, Pallas kernels for 0%

commit v1 on v0

--- a/solution.py
+++ b/solution.py
@@ -3,6 +3,8 @@
 import jax
 import jax.numpy as jnp
 from jax import lax
+from jax.experimental import pallas as pl
+from jax.experimental.pallas import tpu as pltpu
 from jax.sharding import PartitionSpec as P
 
 EH = 64
@@ -116,7 +118,7 @@
     return earlier + later
 
 
-def shards(
+def gathered_shards(
     byte_states,
     enc_gain,
     enc_qkv,
@@ -251,9 +253,463 @@
     return (encoded, latent)
 
 
+MESH = pl.DeviceIdType.MESH
+EDGE = 16
+
+
+def greet(peers):
+    barrier = pltpu.get_barrier_semaphore()
+    for peer in peers:
+        pl.semaphore_signal(barrier, inc=1, device_id=peer, device_id_type=MESH)
+    pl.semaphore_wait(barrier, len(peers))
+
+
+def exchange(values, out_shapes, plan, call_id):
+    n_in, n_out = len(values), len(out_shapes)
+    n_copies = 16
+
+    def kernel(*refs):
+        ins, outs = refs[:n_in], refs[n_in : n_in + n_out]
+        send_sems, recv_sems = refs[n_in + n_out :]
+        rounds = plan()
+        greet([source for source, _, _ in rounds])
+        copies = []
+        for _, target, items in rounds:
+            for in_id, in_view, out_id, out_view in items:
+                copy = pltpu.make_async_remote_copy(
+                    src_ref=in_view(ins[in_id]),
+                    dst_ref=out_view(outs[out_id]),
+                    send_sem=send_sems.at[len(copies)],
+                    recv_sem=recv_sems.at[len(copies)],
+                    device_id=target,
+                    device_id_type=MESH,
+                )
+                copy.start()
+                copies.append(copy)
+        for copy in copies:
+            copy.wait()
+
+    return pl.pallas_call(
+        kernel,
+        out_shape=out_shapes,
+        in_specs=[pl.BlockSpec(memory_space=pl.ANY)] * n_in,
+        out_specs=[pl.BlockSpec(memory_space=pl.ANY)] * n_out,
+        scratch_shapes=[
+            pltpu.SemaphoreType.DMA((n_copies,)),
+            pltpu.SemaphoreType.DMA((n_copies,)),
+        ],
+        compiler_params=pltpu.CompilerParams(collective_id=call_id, has_side_effects=True),
+    )(*values)
+
+
+def whole(ref):
+    return ref
+
+
+def slot(index):
+    return lambda ref: ref.at[index]
+
+
+def seq_peer(index):
+    return {"seq": index}
+
+
+def tp_peer(index):
+    return {"tp": index}
+
+
+def relay(value, count, spread, plane_first, call_id):
+    block = value.shape[1:] if spread else value.shape
+
+    def kernel(value_ref, out_ref, land, send_a, recv_a, send_b, recv_b, own_sem):
+        s, t = lax.axis_index("seq"), lax.axis_index("tp")
+        p, c = s // 2, lax.rem(s, 2)
+
+        def plane(index):
+            return {"seq": 2 * index + c}
+
+        if plane_first:
+            a, b, first, second = p, t, plane, tp_peer
+        else:
+            a, b, first, second = t, p, tp_peer, plane
+        others_a = [lax.rem(a + k, count) for k in range(1, count)]
+        others_b = [lax.rem(b + k, count) for k in range(1, count)]
+        greet([first(i) for i in others_a] + [second(i) for i in others_b])
+        hops = []
+        for k in range(1, count):
+            target = lax.rem(a + k, count)
+            hop = pltpu.make_async_remote_copy(
+                src_ref=value_ref.at[target] if spread else value_ref,
+                dst_ref=land.at[k - 1],
+                send_sem=send_a.at[k - 1],
+                recv_sem=recv_a.at[k - 1],
+                device_id=first(target),
+                device_id_type=MESH,
+            )
+            hop.start()
+            hops.append(hop)
+        onward = []
+        for k in range(count):
+            origin = lax.rem(a + count - k, count)
+            if k == 0:
+                here = value_ref.at[a] if spread else value_ref
+            else:
+                hops[k - 1].wait_recv()
+                here = land.at[k - 1]
+            away = pltpu.make_async_remote_copy(
+                src_ref=here,
+                dst_ref=out_ref.at[b],
+                send_sem=send_b.at[k],
+                recv_sem=recv_b.at[b],
+                device_id=second(origin),
+                device_id_type=MESH,
+            )
+            stay = pltpu.make_async_copy(here, out_ref.at[b], own_sem)
+            onward.append((origin, away, stay))
+
+            @pl.when(origin != b)
+            def _():
+                away.start()
+
+            @pl.when(origin == b)
+            def _():
+                stay.start()
+
+        for q in range(count):
+
+            @pl.when(b != q)
+            def _():
+                pltpu.make_async_remote_copy(
+                    src_ref=land.at[0],
+                    dst_ref=out_ref.at[q],
+                    send_sem=send_b.at[q],
+                    recv_sem=recv_b.at[q],
+                    device_id=second(b),
+                    device_id_type=MESH,
+                ).wait_recv()
+
+        for hop in hops:
+            hop.wait_send()
+        for origin, away, stay in onward:
+
+            @pl.when(origin != b)
+            def _():
+                away.wait_send()
+
+            @pl.when(origin == b)
+            def _():
+                stay.wait()
+
+    return pl.pallas_call(
+        kernel,
+        out_shape=jax.ShapeDtypeStruct((count, *block), value.dtype),
+        in_specs=[pl.BlockSpec(memory_space=pltpu.VMEM)],
+        out_specs=pl.BlockSpec(memory_space=pl.ANY),
+        scratch_shapes=[
+            pltpu.VMEM((count - 1, *block), value.dtype),
+            pltpu.SemaphoreType.DMA((count - 1,)),
+            pltpu.SemaphoreType.DMA((count - 1,)),
+            pltpu.SemaphoreType.DMA((count,)),
+            pltpu.SemaphoreType.DMA((count,)),
+            pltpu.SemaphoreType.DMA,
+        ],
+        compiler_params=pltpu.CompilerParams(collective_id=call_id, has_side_effects=True),
+    )(value)
+
+
+def like(shape, dtype=jnp.bfloat16):
+    return jax.ShapeDtypeStruct(shape, dtype)
+
+
+def halo(projected, byte_states, info):
+    size = lax.axis_size("seq")
+    rows, width = projected.shape[1:]
+    reach = WIN // rows
+
+    def plan():
+        s = lax.axis_index("seq")
+        rounds = []
+        for k in range(1, size):
+            items = []
+            if k <= reach:
+                items.append((0, lambda ref: ref.at[pl.ds(1, 2)], 0, slot(k - 1)))
+            if k == size - 1:
+                items.append((0, lambda ref: ref.at[:, pl.ds(0, EDGE)], 1, whole))
+                items.append((1, lambda ref: ref.at[pl.ds(0, EDGE)], 2, whole))
+            items.append((2, whole, 3, slot(k - 1)))
+            rounds.append(
+                (seq_peer(lax.rem(s + size - k, size)), seq_peer(lax.rem(s + k, size)), items)
+            )
+        return rounds
+
+    return exchange(
+        [projected, byte_states, info],
+        [
+            like((reach, 2, rows, width)),
+            like((3, EDGE, width)),
+            like((EDGE, byte_states.shape[1])),
+            like((size - 1, 8, 128), jnp.int32),
+        ],
+        plan,
+        1,
+    )
+
+
+def turn(values, axis_kind, send_views, out_shapes, call_id, count, by_source=False):
+    def plan():
+        s, t = lax.axis_index("seq"), lax.axis_index("tp")
+        p, c = s // 2, lax.rem(s, 2)
+        rounds = []
+        for k in range(1, count):
+            if axis_kind == "tp":
+                me = t
+                peer = tp_peer
+            else:
+                me = p
+                peer = lambda i: {"seq": 2 * i + c}
+            target = lax.rem(me + k, count)
+            source = lax.rem(me + count - k, count)
+            items = [
+                (i, (lambda ref, v=view, to=target: v(ref, to)), i, slot(me if by_source else k - 1))
+                for i, view in enumerate(send_views)
+            ]
+            rounds.append((peer(source), peer(target), items))
+        return rounds
+
+    return exchange(values, out_shapes, plan, call_id)
+
+
+def swap_cores(value, call_id):
+    def plan():
+        s = lax.axis_index("seq")
+        other = seq_peer(s + 1 - 2 * lax.rem(s, 2))
+        return [(other, other, [(0, whole, 0, whole)])]
+
+    return exchange([value], [like(value.shape, value.dtype)], plan, call_id)[0]
+
+
+def shards(
+    byte_states,
+    enc_gain,
+    enc_qkv,
+    enc_proj_out,
+    starts,
+    counts,
+    lift,
+    cross_kv,
+    latent_gain,
+    lat_qkv,
+    lat_proj_out,
+):
+    size, tp_size = lax.axis_size("seq"), lax.axis_size("tp")
+    s, t = lax.axis_index("seq"), lax.axis_index("tp")
+    pairs = size // 2
+    p, c = s // 2, lax.rem(s, 2)
+    byte_rows = byte_states.shape[0]
+    anchor = s * byte_rows
+    both = [(i, i ^ 1) for i in range(size)]
+    lat_qkv_other = lax.ppermute(lat_qkv, "seq", both)
+    lat_proj_other = lax.ppermute(lat_proj_out, "seq", both)
+    states = byte_states.astype(jnp.float32)
+    normed = rms_scale(states, enc_gain.astype(jnp.float32)).astype(jnp.bfloat16)
+    projected = jnp.einsum(
+        "bd,idc->ibc", normed, enc_qkv, preferred_element_type=jnp.float32
+    ).astype(jnp.bfloat16)
+    patch_count = counts[0]
+    local_starts = starts[0]
+    lanes = lax.broadcasted_iota(jnp.int32, (8, 128), 1)
+    info = jnp.where(lanes == 0, patch_count, jnp.where(lanes == 1, local_starts[0], 0))
+    behind, edge, edge_states, infos = halo(projected, byte_states, info)
+    reach = WIN // byte_rows
+    key_rows = jnp.concatenate(
+        [behind[k, 0] for k in range(reach - 1, -1, -1)] + [projected[1], edge[1]], axis=0
+    )
+    value_rows = jnp.concatenate(
+        [behind[k, 1] for k in range(reach - 1, -1, -1)] + [projected[2], edge[2]], axis=0
+    )
+    query_rows = jnp.concatenate([projected[0], edge[0]], axis=0)
+    total_rows = byte_rows + EDGE
+    head_count = projected.shape[2] // EH
+    scores = jnp.einsum(
+        "qhd,khd->hqk",
+        query_rows.reshape(total_rows, head_count, EH),
+        key_rows.reshape(-1, head_count, EH),
+        preferred_element_type=jnp.float32,
+    ) * (1.0 / math.sqrt(EH))
+    query_pos = anchor + jnp.arange(total_rows, dtype=jnp.int32)
+    key_pos = anchor - WIN + jnp.arange(WIN + total_rows, dtype=jnp.int32)
+    allowed = (
+        (key_pos[None, :] <= query_pos[:, None])
+        & (key_pos[None, :] > query_pos[:, None] - WIN)
+        & (key_pos[None, :] >= 0)
+    )
+    weights = masked_softmax(scores, allowed[None]).astype(jnp.bfloat16)
+    attended = jnp.einsum(
+        "hqk,khd->qhd",
+        weights,
+        value_rows.reshape(-1, head_count, EH),
+        preferred_element_type=jnp.float32,
+    )
+    attended = attended.reshape(total_rows, head_count * EH).astype(jnp.bfloat16)
+    blend = jnp.dot(attended, enc_proj_out, preferred_element_type=jnp.float32).astype(
+        jnp.bfloat16
+    )
+    width = blend.shape[1]
+    share = byte_rows // tp_size
+    tail = jnp.broadcast_to(blend[byte_rows:][None], (tp_size, EDGE, width))
+    blend = jnp.concatenate([blend[:byte_rows].reshape(tp_size, share, width), tail], axis=1)
+    (blends,) = turn(
+        [blend],
+        "tp",
+        [lambda ref, target: ref.at[target]],
+        [like((tp_size - 1, share + EDGE, width))],
+        2,
+        tp_size,
+    )
+    mine = lax.dynamic_index_in_dim(blend, t, 0, keepdims=False).astype(jnp.float32)
+    mine = mine + jnp.sum(blends.astype(jnp.float32), axis=0)
+    my_states = jnp.concatenate(
+        [lax.dynamic_slice_in_dim(byte_states, t * share, share, 0), edge_states], axis=0
+    )
+    mine = (mine + my_states.astype(jnp.float32)).astype(jnp.bfloat16)
+    my_encoded = mine[:share]
+    (encodeds,) = turn(
+        [my_encoded],
+        "tp",
+        [lambda ref, target: ref],
+        [like((tp_size, share, width))],
+        3,
+        tp_size,
+        by_source=True,
+    )
+    tp_ids = jnp.arange(tp_size, dtype=jnp.int32)[:, None, None]
+    encoded = jnp.where(tp_ids == t, my_encoded[None], encodeds).reshape(byte_rows, width)
+    extended = jnp.concatenate([encoded, mine[share : share + SPILL]], axis=0)
+
+    recent = jnp.concatenate([info[None], infos], axis=0)
+    ring = jnp.arange(size, dtype=jnp.int32)
+    from_ring = lax.rem(s - ring + size, size)
+    placed = from_ring[None, :] == ring[:, None]
+    count_list = jnp.sum(jnp.where(placed, recent[None, :, 0, 0], 0), axis=1)
+    offsets = jnp.sum(jnp.where(ring[None, :] < ring[:, None], count_list[None, :], 0), axis=1)
+    next_first = jnp.where(s + 1 < size, recent[size - 1, 0, 1], size * byte_rows)
+
+    slot_total = local_starts.shape[0]
+    slot_ids = jnp.arange(slot_total, dtype=jnp.int32)
+    in_use = slot_ids < patch_count
+    following = jnp.concatenate([local_starts[1:], jnp.zeros((1,), jnp.int32)])
+    patch_end = jnp.where(slot_ids + 1 < patch_count, following, next_first)
+    patches = patch_block(extended, local_starts, patch_end, in_use, anchor, lift, cross_kv)
+
+    def slots_of(core):
+        members = 2 * jnp.arange(pairs, dtype=jnp.int32) + core
+        hit = members[:, None] == ring[None, :]
+        begin = jnp.sum(jnp.where(hit, offsets[None, :], 0), axis=1)
+        used = jnp.sum(jnp.where(hit, count_list[None, :], 0), axis=1)
+        position = (begin[:, None] + slot_ids[None, :]).reshape(-1)
+        return position, (slot_ids[None, :] < used[:, None]).reshape(-1)
+
+    position, rows_used = slots_of(c)
+    other_position, other_used = slots_of(1 - c)
+
+    rows = relay(patches, pairs, False, False, 4).reshape(pairs * slot_total, -1)
+    half = rows.shape[1] // 2
+    full_width = half * size
+    values = rows.astype(jnp.float32)
+    squares = jnp.sum(values * values, axis=-1)
+    gain = lax.dynamic_slice_in_dim(latent_gain, p * 2 * half, 2 * half, 0)
+    geared = (values * gain.astype(jnp.float32)[None]).astype(jnp.bfloat16)
+    low, high = geared[:, :half], geared[:, half:]
+    partial = (
+        jnp.einsum(
+            "pd,idc->ipc", jnp.where(c == 0, low, high), lat_qkv, preferred_element_type=jnp.float32
+        )
+        + jnp.einsum(
+            "pd,idc->ipc",
+            jnp.where(c == 0, high, low),
+            lat_qkv_other,
+            preferred_element_type=jnp.float32,
+        )
+    ).astype(jnp.bfloat16)
+    row_total = rows.shape[0]
+    square_block = jnp.pad(
+        squares.reshape(row_total // 128, 128), ((0, 8 - row_total // 128), (0, 0))
+    )
+    parts, square_parts = turn(
+        [partial, square_block],
+        "pair",
+        [lambda ref, target: ref.at[:, :, pl.ds(pl.multiple_of(target * HD, HD), HD)], lambda ref, target: ref],
+        [like((pairs - 1, 3, row_total, HD)), like((pairs - 1, 8, 128), jnp.float32)],
+        5,
+        pairs,
+    )
+    projected = lax.dynamic_slice_in_dim(partial, p * HD, HD, 2).astype(jnp.float32) + jnp.sum(
+        parts.astype(jnp.float32), axis=0
+    )
+    square_sum = (square_block + jnp.sum(square_parts, axis=0)).reshape(-1)[:row_total]
+    projected = projected * lax.rsqrt(square_sum / full_width + epsilon)[None, :, None]
+    queries = rotate(projected[0][:, None], position)[:, 0].astype(jnp.bfloat16)
+    keys = rotate(projected[1][:, None], position)[:, 0].astype(jnp.bfloat16)
+    key_value = jnp.stack([keys, projected[2].astype(jnp.bfloat16)])
+    key_value_other = swap_cores(key_value, 6)
+    all_keys = jnp.concatenate([key_value[0], key_value_other[0]], axis=0)
+    all_values = jnp.concatenate([key_value[1], key_value_other[1]], axis=0)
+    key_position = jnp.concatenate(
+        [
+            jnp.where(rows_used, position, far_position),
+            jnp.where(other_used, other_position, far_position),
+        ]
+    )
+    scores = jnp.dot(queries, all_keys.T, preferred_element_type=jnp.float32) * (
+        1.0 / math.sqrt(HD)
+    )
+    permitted = key_position[None, :] <= position[:, None]
+    weights = masked_softmax(scores, permitted).astype(jnp.bfloat16)
+    attended = jnp.dot(weights, all_values, preferred_element_type=jnp.float32).astype(
+        jnp.bfloat16
+    )
+    (heads,) = turn(
+        [attended],
+        "pair",
+        [lambda ref, target: ref],
+        [like((pairs, row_total, HD))],
+        7,
+        pairs,
+        by_source=True,
+    )
+    attended = jnp.concatenate(
+        [jnp.where(p == q, attended, heads[q]) for q in range(pairs)], axis=1
+    )
+    own_out = jnp.dot(attended, lat_proj_out, preferred_element_type=jnp.float32)
+    other_out = jnp.dot(attended, lat_proj_other, preferred_element_type=jnp.float32)
+    partials = jnp.concatenate(
+        [jnp.where(c == 0, own_out, other_out), jnp.where(c == 0, other_out, own_out)], axis=1
+    ).astype(jnp.bfloat16)
+    reduced = relay(partials.reshape(pairs, slot_total, -1), pairs, True, True, 8)
+    latent = patches.astype(jnp.float32) + jnp.sum(reduced.astype(jnp.float32), axis=0)
+    latent = jnp.where(in_use[:, None], latent, 0.0).astype(jnp.bfloat16)
+    return (encoded, latent)
+
+
+def fits_pairs(mesh, byte_states, enc_qkv, starts, lat_qkv):
+    size, tp_size = mesh.shape["seq"], mesh.shape["tp"]
+    byte_rows = byte_states.shape[0] // size
+    return (
+        size == 2 * tp_size
+        and WIN % byte_rows == 0
+        and WIN // byte_rows < size
+        and byte_rows % (16 * tp_size) == 0
+        and lat_qkv.shape[2] // tp_size == HD * tp_size
+        and lat_qkv.shape[1] % (128 * size) == 0
+        and starts.shape[1] * tp_size % 128 == 0
+        and starts.shape[1] * tp_size <= 1024
+        and starts.shape[1] % 16 == 0
+        and enc_qkv.shape[2] % (128 * tp_size) == 0
+    )
+
+
 def solution(mesh):
-    return jax.shard_map(
-        shards,
+    specs = dict(
         mesh=mesh,
         in_specs=(
             P("seq", None),
@@ -271,3 +727,9 @@
         out_specs=(P("seq", None), P("seq", "tp")),
         check_vma=False,
     )
+
+    def run(*arrays):
+        paired = fits_pairs(mesh, arrays[0], arrays[2], arrays[4], arrays[9])
+        return jax.shard_map(shards if paired else gathered_shards, **specs)(*arrays)
+
+    return run

time: 189 us -> 163 us (0.86)
  Pallas kernels: 0 us -> 106 us
  waiting for transfers between devices: 55 us -> 0.01 us
  blocking collectives: 53.3 us -> 0 us
  between operations: 17.8 us -> 2.52 us
  other arithmetic: 8.74 us -> 23.1 us
  starting transfers between devices: 12.6 us -> 0.57 us
  matrix products: 27.3 us -> 21.5 us
  loops' own time: 4.55 us -> 0 us
    pallas_call x0 -> x8, Pallas kernels: none -> 106 us  [the longest x6 66.4 us: exchange(): pl.pallas_call(kernel, out_shape=out_shapes, in_specs=[pl.BlockSpec(memor...]
    all_gather x3 -> x0, blocking collectives: 37.7 us -> none  [the longest x1 15.5 us: shards(): full_rows = lax.all_gather(patches, 'tp', axis=1, tiled=True)]
    reduce_scatter x1 -> x0, waiting for transfers between devices: 27.6 us -> none  [shards(): reduced = lax.psum_scatter(partials, 'tp', scatter_dimension=1, tiled=True)]
    psum x1 -> x0, waiting for transfers between devices: 21.6 us -> none  [shards(): lax.psum(jnp.dot(attended, enc_proj_out, preferred_element_type=jnp.float...]
    unnamed x2 -> x0, blocking collectives: 15.6 us -> none
    ppermute x6 -> x2, starting transfers between devices: 12.4 us -> 0.57 us  [the longest x1 0.49 us: shards(): lat_proj_other = lax.ppermute(lat_proj_out, 'seq', both)]
    reduce_sum x1 -> x9, other arithmetic: 0.24 us -> 6.13 us  [the longest x1 1.23 us: shards(): squares = jnp.sum(values * values, axis=-1)]
    ppermute x6 -> x2, waiting for transfers between devices: 5.23 us -> 0.01 us  [the longest x1 0.01 us: shards(): lat_proj_other = lax.ppermute(lat_proj_out, 'seq', both)]
  transfers between devices with their start and end apart: 10 -> 2, of which waited for: 7 -> 0; matrix products, arithmetic and copies ran while one was open for 17% -> 29% of each run, Pallas kernels for 0% -> 53%
where the time goes in v1:
time: 163 us; the launch traced here: 162 us
  Pallas kernels  106 us (65%)
  other arithmetic  23.1 us (14%)
  matrix products  21.5 us (13%)
  local copies, waits for them, and re-layouts  7.35 us (5%)
  between operations  2.52 us (2%)
    pallas_call x6, Pallas kernels, exchange(): pl.pallas_call(kernel, out_shape=out_shapes, in_specs=[pl.BlockSpec(memor...  66.4 us
    pallas_call x2, Pallas kernels, relay(): pl.pallas_call(kernel, out_shape=jax.ShapeDtypeStruct((count, *block), va...  40.1 us
    dot_general x1, matrix products, patch_block(): jnp.dot(extended, cross_kv[0], preferred_element_type=jnp.float32)  3.36 us
  transfers between devices with their start and end apart: 2, of which 0 were waited for; matrix products, arithmetic and copies ran while one was open for 29% of the time, Pallas kernels for 53%

profile of v1, /device:TPU:6, one launch (start us, length us, event | category | flops | bytes accessed | tf_op | source)
XLA Modules:
  0.0 161.6 jit_solution(11871184251364293577)
XLA Ops:
  1.9 0.7 compare_select_fusion.4
  2.6 0.7 convert_element_type.150
  3.3 1.2 fusion.34
  4.5 2.2 %fusion.30.refs_0_ = bf16[3,256,256]{2,1,0:T(8,128)(2,1)S(1)} fusion(bf16[3,1024,256]{2,1,0:T(8,128)(2,1)} %param.13, bf16[256,1024]{1,0:T(8,128)(2,1)} %refs_1_.1, f32[1024]{0:T(1024)S(1)} %convert_element_type.150, f32[256]{0:T(256)S(1)} %add_rsqrt_fusion), kind=kOutput, calls=%fused_computation.32 | convolution fusion | flops 403898368 | bytes 2495488 | tf_op jit(solution)/shard_map/bd,idc->ibc/dot_general | solution.py:515
  6.8 0.7 broadcast_select_fusion.2.refs_2_
  7.5 13.9 %shard_map.122 = (bf16[2,2,256,256]{3,2,1,0:T(8,128)(2,1)}, bf16[3,16,256]{2,1,0:T(8,128)(2,1)}, bf16[16,1024]{1,0:T(8,128)(2,1)}, s32[7,8,128]{2,1,0:T(8,128)}) custom-call(bf16[3,256,256]{2,1,0:T(8,128)(2,1)} %copy-done.1, bf16[256,1024]{1,0:T(8,128)(2,1)} %refs_1_.1, s32[8,128]{1,0:T(8,128)} %broadcast_select_fusion.2.refs_2_), custom_call_target="tpu_custom_call" | custom-call | tf_op jit(solution)/shard_map/pallas_call | solution.py:292
  21.3 1.1 fusion.140
  22.7 0.7 fusion.142
  24.6 0.7 fusion.53
  25.3 2.3 %fusion.144 = (f32[4,272]{1,0:T(4,128)S(1)}, f32[4,272,784]{2,1,0:T(8,128)S(1)}) fusion(f32[4,272,784]{2,1,0:T(8,128)S(1)} %fusion.53, pred[272,784]{1,0:T(8,128)(4,1)S(1)} %and_and_fusion), kind=kOutput, calls=%fused_computation.220 | output fusion | flops 5971727 | bytes 7041536 | tf_op jit(solution)/shard_map/sub | solution.py:55
  27.6 0.8 fusion.31
  29.1 0.9 pad_maximum_fusion.refs_0_
  30.0 16.0 %shard_map.123 = bf16[3,80,1024]{2,1,0:T(8,128)(2,1)} custom-call(bf16[4,80,1024]{2,1,0:T(8,128)(2,1)} %pad_maximum_fusion.refs_0_), custom_call_target="tpu_custom_call" | custom-call | tf_op jit(solution)/shard_map/pallas_call | solution.py:292
  46.0 1.1 convert_reduce_fusion.2
  47.1 0.9 constant_dynamic-slice_fusion
  48.1 0.7 slice.152.refs_0_
  48.9 16.2 %shard_map.124 = bf16[4,64,1024]{2,1,0:T(8,128)(2,1)} custom-call(bf16[64,1024]{1,0:T(8,128)(2,1)} %slice.152.refs_0_), custom_call_target="tpu_custom_call" | custom-call | tf_op jit(solution)/shard_map/pallas_call | solution.py:292
  65.0 1.2 broadcast_select_fusion
  66.2 3.4 %fusion.23 = bf16[33,8,8,128]{3,2,1,0:T(8,128)(2,1)} fusion(bf16[2,1024,1024]{2,1,0:T(8,128)(2,1)} %param.18, bf16[8,1024]{1,0:T(8,128)(2,1)S(1)} %slice.153, bf16[256,1024]{1,0:T(8,128)(2,1)S(1)} %bitcast.150), kind=kOutput, calls=%fused_computation.28 | convolution fusion | flops 554999808 | bytes 3178496 | tf_op jit(solution)/shard_map/dot_general | solution.py:90
  69.6 1.6 fusion.26
  71.2 0.6 slice.126
  72.8 0.7 fusion.33
  73.6 2.5 %fusion.145 = (f32[8,64]{1,0:T(8,128)S(1)}, f32[8,64,264]{2,1,0:T(8,128)}) fusion(bf16[33,8,8,128]{3,2,1,0:T(8,128)(2,1)} %fusion.23, pred[64,264]{1,0:T(8,128)(4,1)S(1)} %and_or_fusion, f32[64,1024]{1,0:T(8,128)S(1)} %fusion.33), kind=kOutput, calls=%fused_computation.221 | convolution fusion | flops 35344648 | bytes 1362432 | tf_op jit(solution)/shard_map/sub | solution.py:55
  76.0 1.5 convolution_bitcast_fusion
  77.5 0.7 fusion.67.value_ref
  78.2 18.6 %shard_map.125 = bf16[4,64,1024]{2,1,0:T(8,128)(2,1)} custom-call(bf16[64,1024]{1,0:T(8,128)(2,1)} %fusion.67.value_ref), custom_call_target="tpu_custom_call" | custom-call | tf_op jit(solution)/shard_map/pallas_call | solution.py:403
  96.8 1.2 multiply_reduce_fusion
  99.3 0.6 pad.4.refs_1_
  99.9 0.7 dynamic-slice_convert_fusion
  100.6 1.1 fusion.37
  101.8 2.0 %fusion.69 = f32[256,3,512]{2,0,1:T(8,128)S(1)} fusion(bf16[3,512,512]{2,1,0:T(8,128)(2,1)} %param.20, pred[]{:T(512)S(6)} %eq.102, bf16[256,1024]{1,0:T(8,128)(2,1)S(1)} %fusion.37), kind=kOutput, calls=%fused_computation.94 | convolution fusion | flops 402784256 | bytes 3670017 | tf_op jit(solution)/shard_map/pd,idc->ipc/dot_general | solution.py:624
  103.8 2.9 %add_convert_fusion = bf16[256,3,512]{2,0,1:T(8,128)(2,1)} fusion(f32[256,3,512]{2,0,1:T(8,128)S(1)} %fusion.69, bf16[3,512,512]{2,1,0:T(8,128)(2,1)} %collective-permute-done, pred[]{:T(512)S(6)} %eq.102, bf16[256,1024]{1,0:T(8,128)(2,1)S(1)} %fusion.37), kind=kOutput, calls=%fused_computation.16 | convolution fusion | flops 403570688 | bytes 4456449 | tf_op jit(solution)/shard_map/pd,idc->ipc/dot_general | solution.py:627
  106.7 11.4 %shard_map.126 = (bf16[3,3,256,128]{3,2,1,0:T(8,128)(2,1)}, f32[3,8,128]{2,1,0:T(8,128)}) custom-call(bf16[3,256,512]{2,1,0:T(8,128)(2,1)} %bitcast.145, f32[8,128]{1,0:T(8,128)} %pad.4.refs_1_), custom_call_target="tpu_custom_call" | custom-call | tf_op jit(solution)/shard_map/pallas_call | solution.py:292
  118.1 0.7 reduce_sum.157
  118.8 1.2 convert_reduce_fusion
  120.0 1.0 fusion.62
  121.1 0.6 fusion.96
  122.5 0.7 pad_maximum_fusion.8.refs_0_
  123.1 2.0 %shard_map.127 = bf16[2,256,128]{2,1,0:T(8,128)(2,1)} custom-call(bf16[2,256,128]{2,1,0:T(8,128)(2,1)} %pad_maximum_fusion.8.refs_0_), custom_call_target="tpu_custom_call" | custom-call | tf_op jit(solution)/shard_map/pallas_call | solution.py:292
  125.1 0.9 slice_bitcast_fusion.2
  126.6 0.9 convolution_convert_fusion.2.refs_0_
  127.6 7.1 %shard_map.128 = bf16[4,256,128]{2,1,0:T(8,128)(2,1)} custom-call(bf16[256,128]{1,0:T(8,128)(2,1)} %convolution_convert_fusion.2.refs_0_), custom_call_target="tpu_custom_call" | custom-call | tf_op jit(solution)/shard_map/pallas_call | solution.py:292
  134.6 1.0 bitcast_select_fusion.3
  136.0 1.4 select_convert_fusion.1
  137.3 0.9 pad_maximum_fusion.2.value_ref
  138.2 21.5 %shard_map.129 = bf16[4,64,1024]{2,1,0:T(8,128)(2,1)} custom-call(bf16[4,64,1024]{2,1,0:T(8,128)(2,1)} %pad_maximum_fusion.2.value_ref), custom_call_target="tpu_custom_call" | custom-call | tf_op jit(solution)/shard_map/pallas_call | solution.py:403
  159.7 1.1 convert_reduce_fusion.1
  160.8 0.7 select_convert_fusion.2
  (86 shorter events, 6.1 us)
Async XLA Ops:
  0.6 72.1 %copy-start = (bf16[1024,1024]{1,0:T(8,128)(2,1)S(1)}, bf16[1024,1024]{1,0:T(8,128)(2,1)}, u32[]{:S(2)}) copy-start(bf16[1024,1024]{1,0:T(8,128)(2,1)} %param.17) | copy-start | bytes 6291460
  0.6 103.1 %collective-permute-start = (bf16[3,512,512]{2,1,0:T(8,128)(2,1)}, bf16[3,512,512]{2,1,0:T(8,128)(2,1)}, u32[]{:S(2)}, u32[]{:S(2)}) collective-permute-start(bf16[3,512,512]{2,1,0:T(8,128)(2,1)} %param.20), channel_id=1, source_target_pairs={{0,4},{4,0},{8,12},{12,8},{16,20},{20,16},{24,28},{28,24},{1,5},{5... | collective-permute-start | bytes 4718600 | tf_op jit(solution)/shard_map/ppermute | solution.py:511
  0.7 135.2 %collective-permute-start.1 = (bf16[512,512]{1,0:T(8,128)(2,1)}, bf16[512,512]{1,0:T(8,128)(2,1)}, u32[]{:S(2)}, u32[]{:S(2)}) collective-permute-start(bf16[512,512]{1,0:T(8,128)(2,1)} %param.21), channel_id=1, source_target_pairs={{0,4},{4,0},{8,12},{12,8},{16,20},{20,16},{24,28},{28,24},{1,5},{5... | collective-permute-start | bytes 1572872 | tf_op jit(solution)/shard_map/ppermute | solution.py:512
  6.7 0.8 copy-start.1
  27.6 1.0 copy-start.3
  29.0 19.0 %copy-start.5 = (bf16[16,1024]{1,0:T(8,128)(2,1)S(1)}, bf16[16,1024]{1,0:T(8,128)(2,1)}, u32[]{:S(2)}) copy-start(bf16[16,1024]{1,0:T(8,128)(2,1)} %get-tuple-element.10) | copy-start | bytes 98308
  30.0 18.8 %copy-start.7 = (s32[1,64]{1,0:T(1,128)S(1)}, s32[1,64]{1,0:T(1,128)}, u32[]{:S(2)}) copy-start(s32[1,64]{1,0:T(1,128)} %param.15) | copy-start | bytes 772
  66.2 6.5 %copy-start.4 = (bf16[4,64,1024]{2,1,0:T(8,128)(2,1)}, bf16[4,64,1024]{2,1,0:T(8,128)(2,1)S(1)}, u32[]{:S(2)}) copy-start(bf16[4,64,1024]{2,1,0:T(8,128)(2,1)S(1)} %broadcast_select_fusion) | copy-start | bytes 1572868
  66.2 3.4 %copy-start.8 = (bf16[2,1024,1024]{2,1,0:T(8,128)(2,1)S(1)}, bf16[2,1024,1024]{2,1,0:T(8,128)(2,1)}, u32[]{:S(2)}) copy-start(bf16[2,1024,1024]{2,1,0:T(8,128)(2,1)} %param.18) | copy-start | bytes 12582916
  69.6 1.6 copy-start.6
  73.4 2.6 %copy-start.10 = (bf16[33,8,8,128]{3,2,1,0:T(8,128)(2,1)S(1)}, bf16[33,8,8,128]{3,2,1,0:T(8,128)(2,1)}, u32[]{:S(2)}) copy-start(bf16[33,8,8,128]{3,2,1,0:T(8,128)(2,1)} %fusion.26) | copy-start | bytes 1622020
  126.4 9.3 %copy-start.9 = (bf16[512,512]{1,0:T(8,128)(2,1)S(1)}, bf16[512,512]{1,0:T(8,128)(2,1)}, u32[]{:S(2)}) copy-start(bf16[512,512]{1,0:T(8,128)(2,1)} %param.21) | copy-start | bytes 1572868
  135.9 24.9 %copy-start.2 = (bf16[64,1024]{1,0:T(8,128)(2,1)S(1)}, bf16[64,1024]{1,0:T(8,128)(2,1)}, u32[]{:S(2)}) copy-start(bf16[64,1024]{1,0:T(8,128)(2,1)} %fusion.67.value_ref) | copy-start | bytes 393220

commit v2 on v1

--- a/solution.py
+++ b/solution.py
@@ -479,6 +479,213 @@
     return exchange(values, out_shapes, plan, call_id)
 
 
+def blend_and_patch(attended, proj, byte_states, edge_states, bounds, used, lift, cross_kv, call_id):
+    count = lax.axis_size("tp")
+    byte_rows, width = byte_states.shape
+    share = byte_rows // count
+    chunks = 2
+    piece = share // chunks
+    slots = bounds[0].shape[0]
+    columns = lift.shape[1]
+    total_rows = byte_rows + EDGE
+
+    def kernel(
+        att_ref, proj_ref, states_ref, edge_ref, lo_ref, hi_ref, used_ref, lift_hbm, cross_hbm,
+        full_ref, patch_ref,
+        sends, lands, tail_send, tail_land, blocks, lift_ref, cross_ref, pooled_ref,
+        load_sems, rs_send, rs_recv, tail_s, tail_r, up_send, down_send, ag_recv,
+    ):
+        t = lax.axis_index("tp")
+        loads = [
+            pltpu.make_async_copy(lift_hbm, lift_ref, load_sems.at[0]),
+            pltpu.make_async_copy(cross_hbm, cross_ref, load_sems.at[1]),
+        ]
+        for load in loads:
+            load.start()
+        blend = jnp.dot(att_ref[...], proj_ref[...], preferred_element_type=jnp.float32).astype(
+            jnp.bfloat16
+        )
+        for q in range(count):
+            for h in range(chunks):
+                begin = q * share + h * piece
+                sends[q, h] = blend[begin : begin + piece]
+        tail_send[...] = blend[byte_rows:]
+        greet([tp_peer(lax.rem(t + k, count)) for k in range(1, count)])
+        scatter = [[], []]
+        for h in range(chunks):
+            for k in range(1, count):
+                target = lax.rem(t + k, count)
+                copy = pltpu.make_async_remote_copy(
+                    src_ref=sends.at[target, h],
+                    dst_ref=lands.at[h, k - 1],
+                    send_sem=rs_send.at[h, k - 1],
+                    recv_sem=rs_recv.at[h, k - 1],
+                    device_id=tp_peer(target),
+                    device_id_type=MESH,
+                )
+                copy.start()
+                scatter[h].append(copy)
+        tails = []
+        for k in range(1, count):
+            copy = pltpu.make_async_remote_copy(
+                src_ref=tail_send,
+                dst_ref=tail_land.at[k - 1],
+                send_sem=tail_s.at[k - 1],
+                recv_sem=tail_r.at[k - 1],
+                device_id=tp_peer(lax.rem(t + k, count)),
+                device_id_type=MESH,
+            )
+            copy.start()
+            tails.append(copy)
+
+        def pass_on(origin, h, up):
+            step = 1 if up else -1
+            return pltpu.make_async_remote_copy(
+                src_ref=blocks.at[origin, h],
+                dst_ref=blocks.at[origin, h],
+                send_sem=(up_send if up else down_send).at[origin, h],
+                recv_sem=ag_recv.at[origin, h],
+                device_id=tp_peer(lax.rem(t + step + count, count)),
+                device_id_type=MESH,
+            )
+
+        for h in range(chunks):
+            for copy in scatter[h]:
+                copy.wait_recv()
+            total = sends[t, h].astype(jnp.float32)
+            for k in range(count - 1):
+                total = total + lands[h, k].astype(jnp.float32)
+            rows = pl.ds(pl.multiple_of(t * share + h * piece, piece), piece)
+            blocks[t, h] = (states_ref[rows].astype(jnp.float32) + total).astype(jnp.bfloat16)
+
+            @pl.when(t < count - 1)
+            def _():
+                pass_on(t, h, True).start()
+
+            @pl.when(t > 0)
+            def _():
+                pass_on(t, h, False).start()
+
+        for copy in tails:
+            copy.wait_recv()
+        total = tail_send[...].astype(jnp.float32)
+        for k in range(count - 1):
+            total = total + tail_land[k].astype(jnp.float32)
+        full_ref[byte_rows:] = (edge_ref[...].astype(jnp.float32) + total).astype(jnp.bfloat16)
+
+        for d in range(1, count):
+            for h in range(chunks):
+
+                @pl.when(t - d >= 0)
+                def _():
+                    pass_on(t - d, h, True).wait_recv()
+
+                    @pl.when(t < count - 1)
+                    def _():
+                        pass_on(t - d, h, True).start()
+
+                @pl.when(t + d < count)
+                def _():
+                    pass_on(t + d, h, False).wait_recv()
+
+                    @pl.when(t > 0)
+                    def _():
+                        pass_on(t + d, h, False).start()
+
+        for q in range(count):
+            for h in range(chunks):
+                begin = q * share + h * piece
+                full_ref[begin : begin + piece] = blocks[q, h]
+        for load in loads:
+            load.wait()
+
+        where_at = lax.broadcasted_iota(jnp.int32, (slots, total_rows), 1)
+        allowed = (where_at >= lo_ref[...]) & (where_at < hi_ref[...])
+        in_use = used_ref[...] > 0.0
+        member = jnp.where(allowed & in_use, 1.0, 0.0)
+        lengths = jnp.maximum(jnp.sum(member, axis=1, keepdims=True), 1.0)
+        totals = jnp.dot(
+            member.astype(jnp.bfloat16), full_ref[...], preferred_element_type=jnp.float32
+        )
+        pooled_ref[...] = (totals / lengths).astype(jnp.bfloat16)
+        group = 2 * HD
+
+        def heads(i, carry):
+            cols = pl.ds(pl.multiple_of(i * group, group), group)
+            rows = full_ref[...]
+            lifted = jnp.dot(pooled_ref[...], lift_ref[:, cols], preferred_element_type=jnp.float32)
+            keys = jnp.dot(rows, cross_ref[0, :, cols], preferred_element_type=jnp.float32).astype(
+                jnp.bfloat16
+            )
+            values = jnp.dot(
+                rows, cross_ref[1, :, cols], preferred_element_type=jnp.float32
+            ).astype(jnp.bfloat16)
+            queries = lifted.astype(jnp.bfloat16)
+            crossed = []
+            for j in range(2):
+                lanes = slice(j * HD, (j + 1) * HD)
+                scores = lax.dot_general(
+                    queries[:, lanes],
+                    keys[:, lanes],
+                    (((1,), (1,)), ((), ())),
+                    preferred_element_type=jnp.float32,
+                ) * (1.0 / math.sqrt(HD))
+                weights = masked_softmax(scores, allowed).astype(jnp.bfloat16)
+                crossed.append(
+                    jnp.dot(weights, values[:, lanes], preferred_element_type=jnp.float32)
+                )
+            patch = lifted + jnp.concatenate(crossed, axis=1)
+            patch_ref[:, cols] = jnp.where(in_use, patch, 0.0).astype(jnp.bfloat16)
+            return carry
+
+        lax.fori_loop(0, columns // group, heads, 0)
+
+        for h in range(chunks):
+            for copy in scatter[h]:
+                copy.wait_send()
+        for copy in tails:
+            copy.wait_send()
+        for q in range(count):
+            for h in range(chunks):
+
+                @pl.when((q <= t) & (t < count - 1))
+                def _():
+                    pass_on(q, h, True).wait_send()
+
+                @pl.when((q >= t) & (t > 0))
+                def _():
+                    pass_on(q, h, False).wait_send()
+
+    vmem = pl.BlockSpec(memory_space=pltpu.VMEM)
+    hbm = pl.BlockSpec(memory_space=pl.ANY)
+    dma = pltpu.SemaphoreType.DMA
+    return pl.pallas_call(
+        kernel,
+        out_shape=[like((total_rows, width)), like((slots, columns))],
+        in_specs=[vmem] * 7 + [hbm] * 2,
+        out_specs=[vmem, vmem],
+        scratch_shapes=[
+            pltpu.VMEM((count, chunks, piece, width), jnp.bfloat16),
+            pltpu.VMEM((chunks, count - 1, piece, width), jnp.bfloat16),
+            pltpu.VMEM((EDGE, width), jnp.bfloat16),
+            pltpu.VMEM((count - 1, EDGE, width), jnp.bfloat16),
+            pltpu.VMEM((count, chunks, piece, width), jnp.bfloat16),
+            pltpu.VMEM(lift.shape, lift.dtype),
+            pltpu.VMEM(cross_kv.shape, cross_kv.dtype),
+            pltpu.VMEM((slots, width), jnp.bfloat16),
+            dma((2,)),
+            dma((chunks, count - 1)),
+            dma((chunks, count - 1)),
+            dma((count - 1,)),
+            dma((count - 1,)),
+            dma((count, chunks)),
+            dma((count, chunks)),
+            dma((count, chunks)),
+        ],
+        compiler_params=pltpu.CompilerParams(collective_id=call_id, has_side_effects=True),
+    )(attended, proj, byte_states, edge_states, *bounds, used, lift, cross_kv)
+
+
 def swap_cores(value, call_id):
     def plan():
         s = lax.axis_index("seq")
@@ -551,41 +758,6 @@
         preferred_element_type=jnp.float32,
     )
     attended = attended.reshape(total_rows, head_count * EH).astype(jnp.bfloat16)
-    blend = jnp.dot(attended, enc_proj_out, preferred_element_type=jnp.float32).astype(
-        jnp.bfloat16
-    )
-    width = blend.shape[1]
-    share = byte_rows // tp_size
-    tail = jnp.broadcast_to(blend[byte_rows:][None], (tp_size, EDGE, width))
-    blend = jnp.concatenate([blend[:byte_rows].reshape(tp_size, share, width), tail], axis=1)
-    (blends,) = turn(
-        [blend],
-        "tp",
-        [lambda ref, target: ref.at[target]],
-        [like((tp_size - 1, share + EDGE, width))],
-        2,
-        tp_size,
-    )
-    mine = lax.dynamic_index_in_dim(blend, t, 0, keepdims=False).astype(jnp.float32)
-    mine = mine + jnp.sum(blends.astype(jnp.float32), axis=0)
-    my_states = jnp.concatenate(
-        [lax.dynamic_slice_in_dim(byte_states, t * share, share, 0), edge_states], axis=0
-    )
-    mine = (mine + my_states.astype(jnp.float32)).astype(jnp.bfloat16)
-    my_encoded = mine[:share]
-    (encodeds,) = turn(
-        [my_encoded],
-        "tp",
-        [lambda ref, target: ref],
-        [like((tp_size, share, width))],
-        3,
-        tp_size,
-        by_source=True,
-    )
-    tp_ids = jnp.arange(tp_size, dtype=jnp.int32)[:, None, None]
-    encoded = jnp.where(tp_ids == t, my_encoded[None], encodeds).reshape(byte_rows, width)
-    extended = jnp.concatenate([encoded, mine[share : share + SPILL]], axis=0)
-
     recent = jnp.concatenate([info[None], infos], axis=0)
     ring = jnp.arange(size, dtype=jnp.int32)
     from_ring = lax.rem(s - ring + size, size)
@@ -599,7 +771,21 @@
     in_use = slot_ids < patch_count
     following = jnp.concatenate([local_starts[1:], jnp.zeros((1,), jnp.int32)])
     patch_end = jnp.where(slot_ids + 1 < patch_count, following, next_first)
-    patches = patch_block(extended, local_starts, patch_end, in_use, anchor, lift, cross_kv)
+    lower = jnp.where(in_use, local_starts - anchor, 0)[:, None]
+    upper = jnp.where(in_use, patch_end - anchor, 1)[:, None]
+    used_rows = in_use.astype(jnp.float32)[:, None]
+    extended, patches = blend_and_patch(
+        attended,
+        enc_proj_out,
+        byte_states,
+        edge_states,
+        (lower, upper),
+        used_rows,
+        lift,
+        cross_kv,
+        2,
+    )
+    encoded = extended[:byte_rows]
 
     def slots_of(core):
         members = 2 * jnp.arange(pairs, dtype=jnp.int32) + core
@@ -698,7 +884,7 @@
         size == 2 * tp_size
         and WIN % byte_rows == 0
         and WIN // byte_rows < size
-        and byte_rows % (16 * tp_size) == 0
+        and byte_rows % (32 * tp_size) == 0
         and lat_qkv.shape[2] // tp_size == HD * tp_size
         and lat_qkv.shape[1] % (128 * size) == 0
         and starts.shape[1] * tp_size % 128 == 0

time: 163 us -> 152 us (0.933)
  matrix products: 21.5 us -> 9.66 us
  Pallas kernels: 106 us -> 109 us
  other arithmetic: 23.1 us -> 20.8 us
  local copies, waits for them, and re-layouts: 7.35 us -> 9 us
    pallas_call x0 -> x1, Pallas kernels: none -> 37.8 us  [blend_and_patch(): pl.pallas_call(kernel, out_shape=[like((total_rows, width)), like((slots,...]
    pallas_call x6 -> x4, Pallas kernels: 66.4 us -> 33.7 us  [exchange(): pl.pallas_call(kernel, out_shape=out_shapes, in_specs=[pl.BlockSpec(memor...]
    dot_general x5 -> x0, matrix products: 7.41 us -> none  [the longest x1 3.36 us: patch_block(): jnp.dot(extended, cross_kv[0], preferred_element_type=jnp.float32)]
    pallas_call x2, Pallas kernels: 40.1 us -> 37.3 us  [relay(): pl.pallas_call(kernel, out_shape=jax.ShapeDtypeStruct((count, *block), va...]
    sub x1 -> x0, matrix products: 2.47 us -> none  [masked_softmax(): raised = jnp.where(allowed, jnp.exp(scores - largest), 0.0)]
  transfers between devices with their start and end apart: 2 -> 2, of which waited for: 0 -> 0; matrix products, arithmetic and copies ran while one was open for 29% -> 23% of each run, Pallas kernels for 53% -> 57%
where the time goes in v2:
time: 152 us; the launch traced here: 151 us
  Pallas kernels  109 us (72%)
  other arithmetic  20.8 us (14%)
  matrix products  9.66 us (6%)
  local copies, waits for them, and re-layouts  9 us (6%)
  between operations  2.34 us (2%)
    pallas_call x1, Pallas kernels, blend_and_patch(): pl.pallas_call(kernel, out_shape=[like((total_rows, width)), like((slots,...  37.8 us
    pallas_call x2, Pallas kernels, relay(): pl.pallas_call(kernel, out_shape=jax.ShapeDtypeStruct((count, *block), va...  37.3 us
    pallas_call x4, Pallas kernels, exchange(): pl.pallas_call(kernel, out_shape=out_shapes, in_specs=[pl.BlockSpec(memor...  33.7 us
  transfers between devices with their start and end apart: 2, of which 0 were waited for; matrix products, arithmetic and copies ran while one was open for 23% of the time, Pallas kernels for 57%

profile of v2, /device:TPU:6, one launch (start us, length us, event | category | flops | bytes accessed | tf_op | source)
XLA Modules:
  0.0 151.1 jit_solution(743696625487104687)
XLA Ops:
  0.7 0.5 collective-permute-start.1
  1.3 0.7 subtract_bitcast_fusion
  1.9 0.7 slice_bitcast_fusion.4
  3.3 0.7 compare_select_fusion.3
  4.0 0.7 convert_element_type.118
  4.7 1.2 fusion.9
  5.9 1.7 %fusion.7.refs_0_ = bf16[3,256,256]{2,1,0:T(8,128)(2,1)S(1)} fusion(bf16[3,1024,256]{2,1,0:T(8,128)(2,1)S(1)} %copy-done, bf16[256,1024]{1,0:T(8,128)(2,1)} %states_ref.1, f32[1024]{0:T(1024)S(1)} %convert_element_type.118, f32[256]{0:T(256)S(1)} %add_rsqrt_fusion), kind=kOutput, calls=%fused_computation.15 | convolution fusion | flops 403898368 | bytes 2495488 | tf_op jit(solution)/shard_map/bd,idc->ibc/dot_general | solution.py:722
  7.6 0.7 broadcast_select_fusion.1.refs_2_
  8.3 13.9 %shard_map.122 = (bf16[2,2,256,256]{3,2,1,0:T(8,128)(2,1)}, bf16[3,16,256]{2,1,0:T(8,128)(2,1)}, bf16[16,1024]{1,0:T(8,128)(2,1)}, s32[7,8,128]{2,1,0:T(8,128)}) custom-call(bf16[3,256,256]{2,1,0:T(8,128)(2,1)} %copy-done.2, bf16[256,1024]{1,0:T(8,128)(2,1)} %states_ref.1, s32[8,128]{1,0:T(8,128)} %broadcast_select_fusion.1.refs_2_), custom_call_target="tpu_custom_call" | custom-call | tf_op jit(solution)/shard_map/pallas_call | solution.py:292
  22.2 1.1 fusion.87
  23.5 0.7 fusion.89
  25.2 0.3 and_and_fusion
  25.5 0.7 fusion.24
  26.2 2.3 %fusion.91 = (f32[4,272]{1,0:T(4,128)S(1)}, f32[4,272,784]{2,1,0:T(8,128)S(1)}) fusion(f32[4,272,784]{2,1,0:T(8,128)S(1)} %fusion.24, pred[272,784]{1,0:T(8,128)(4,1)S(1)} %and_and_fusion), kind=kOutput, calls=%fused_computation.166 | output fusion | flops 5971727 | bytes 7041536 | tf_op jit(solution)/shard_map/sub | solution.py:55
  28.5 0.8 fusion.8
  29.3 0.8 copy.75.att_ref
  30.1 0.6 slice.108
  31.0 0.6 fusion.72.used_ref
  32.2 0.6 subtract_select_fusion
  32.9 37.8 %shard_map.123 = (bf16[272,1024]{1,0:T(8,128)(2,1)}, bf16[64,1024]{1,0:T(8,128)(2,1)}) custom-call(bf16[272,256]{1,0:T(8,128)(2,1)} %copy.75.att_ref, bf16[256,1024]{1,0:T(8,128)(2,1)} %proj_ref.1, bf16[256,1024]{1,0:T(8,128)(2,1)} %states_ref.1, bf16[16,1024]{1,0:T(8,128)(2,1)} %get-tuple-element.12.edge_ref, s32[64,1]{1,0:T(8,128)} %get-tuple-element.53.lo_ref, ...), custom_call_target="tpu_custom_call" | custom-call | tf_op jit(solution)/shard_map/pallas_call | solution.py:662
  70.6 15.1 %shard_map.124 = bf16[4,64,1024]{2,1,0:T(8,128)(2,1)} custom-call(bf16[64,1024]{1,0:T(8,128)(2,1)} %get-tuple-element.15.value_ref), custom_call_target="tpu_custom_call" | custom-call | tf_op jit(solution)/shard_map/pallas_call | solution.py:403
  85.8 1.2 multiply_reduce_fusion
  88.2 1.9 %slice.109 = bf16[256,1024]{1,0:T(8,128)(2,1)} slice(bf16[272,1024]{1,0:T(8,128)(2,1)} %get-tuple-element.14), slice={[0:256], [0:1024]} | slice | bytes 1048576 | tf_op jit(solution)/shard_map/slice | solution.py:788
  90.1 0.6 pad.4.refs_1_
  90.7 0.7 dynamic-slice_convert_fusion
  91.4 1.1 fusion.12
  92.6 0.6 fusion.35
  93.2 2.9 %add_convert_fusion = bf16[256,3,512]{2,0,1:T(8,128)(2,1)} fusion(f32[256,3,512]{2,0,1:T(8,128)S(1)} %fusion.35, bf16[3,512,512]{2,1,0:T(8,128)(2,1)} %collective-permute-done, pred[]{:T(512)S(6)} %eq.79, bf16[256,1024]{1,0:T(8,128)(2,1)S(1)} %fusion.12), kind=kOutput, calls=%fused_computation.9 | convolution fusion | flops 403570688 | bytes 4456449 | tf_op jit(solution)/shard_map/pd,idc->ipc/dot_general | solution.py:813
  96.1 10.9 %shard_map.125 = (bf16[3,3,256,128]{3,2,1,0:T(8,128)(2,1)}, f32[3,8,128]{2,1,0:T(8,128)}) custom-call(bf16[3,256,512]{2,1,0:T(8,128)(2,1)} %bitcast.82, f32[8,128]{1,0:T(8,128)} %pad.4.refs_1_), custom_call_target="tpu_custom_call" | custom-call | tf_op jit(solution)/shard_map/pallas_call | solution.py:292
  106.9 0.7 reduce_sum.127
  107.7 1.2 convert_reduce_fusion
  108.9 1.0 fusion.33
  109.9 0.6 fusion.60
  110.8 0.6 fusion.57
  111.3 0.7 pad_maximum_fusion.2.refs_0_
  112.0 2.0 %shard_map.126 = bf16[2,256,128]{2,1,0:T(8,128)(2,1)} custom-call(bf16[2,256,128]{2,1,0:T(8,128)(2,1)} %pad_maximum_fusion.2.refs_0_), custom_call_target="tpu_custom_call" | custom-call | tf_op jit(solution)/shard_map/pallas_call | solution.py:292
  114.0 0.9 slice_bitcast_fusion.2
  114.9 0.4 fusion.92
  115.2 0.3 fusion.32
  115.5 1.0 convolution_convert_fusion.1.refs_0_
  116.5 7.1 %shard_map.127 = bf16[4,256,128]{2,1,0:T(8,128)(2,1)} custom-call(bf16[256,128]{1,0:T(8,128)(2,1)} %convolution_convert_fusion.1.refs_0_), custom_call_target="tpu_custom_call" | custom-call | tf_op jit(solution)/shard_map/pallas_call | solution.py:292
  123.5 1.0 bitcast_select_fusion.3
  124.5 0.3 fusion.71
  124.8 1.3 select_convert_fusion.1
  126.2 0.9 pad_maximum_fusion.value_ref
  127.1 22.2 %shard_map.128 = bf16[4,64,1024]{2,1,0:T(8,128)(2,1)} custom-call(bf16[4,64,1024]{2,1,0:T(8,128)(2,1)} %pad_maximum_fusion.value_ref), custom_call_target="tpu_custom_call" | custom-call | tf_op jit(solution)/shard_map/pallas_call | solution.py:403
  149.2 1.1 convert_reduce_fusion.1
  150.4 0.7 select_convert_fusion.2
  (59 shorter events, 3.0 us)
Async XLA Ops:
  0.6 5.3 %copy-start = (bf16[3,1024,256]{2,1,0:T(8,128)(2,1)S(1)}, bf16[3,1024,256]{2,1,0:T(8,128)(2,1)}, u32[]{:S(2)}) copy-start(bf16[3,1024,256]{2,1,0:T(8,128)(2,1)} %param.13) | copy-start | bytes 4718596
  0.6 92.5 %collective-permute-start = (bf16[3,512,512]{2,1,0:T(8,128)(2,1)}, bf16[3,512,512]{2,1,0:T(8,128)(2,1)}, u32[]{:S(2)}, u32[]{:S(2)}) collective-permute-start(bf16[3,512,512]{2,1,0:T(8,128)(2,1)} %param.20), channel_id=1, source_target_pairs={{0,4},{4,0},{8,12},{12,8},{16,20},{20,16},{24,28},{28,24},{1,5},{5... | collective-permute-start | bytes 4718600 | tf_op jit(solution)/shard_map/ppermute | solution.py:718
  0.7 124.1 %collective-permute-start.1 = (bf16[512,512]{1,0:T(8,128)(2,1)}, bf16[512,512]{1,0:T(8,128)(2,1)}, u32[]{:S(2)}, u32[]{:S(2)}) collective-permute-start(bf16[512,512]{1,0:T(8,128)(2,1)} %param.21), channel_id=1, source_target_pairs={{0,4},{4,0},{8,12},{12,8},{16,20},{20,16},{24,28},{28,24},{1,5},{5... | collective-permute-start | bytes 1572872 | tf_op jit(solution)/shard_map/ppermute | solution.py:719
  7.6 0.8 copy-start.2
  28.5 1.6 %copy-start.4 = (s32[7,8,128]{2,1,0:T(8,128)S(1)}, s32[7,8,128]{2,1,0:T(8,128)}, u32[]{:S(2)}) copy-start(s32[7,8,128]{2,1,0:T(8,128)} %get-tuple-element.13) | copy-start | bytes 86020
  32.9 59.7 %copy-start.1 = (bf16[3,512,512]{2,1,0:T(8,128)(2,1)S(1)}, bf16[3,512,512]{2,1,0:T(8,128)(2,1)}, u32[]{:S(2)}) copy-start(bf16[3,512,512]{2,1,0:T(8,128)(2,1)} %param.20) | copy-start | bytes 4718596
  109.9 14.6 %copy-start.5 = (bf16[512,512]{1,0:T(8,128)(2,1)S(1)}, bf16[512,512]{1,0:T(8,128)(2,1)}, u32[]{:S(2)}) copy-start(bf16[512,512]{1,0:T(8,128)(2,1)} %param.21) | copy-start | bytes 1572868
  116.5 33.9 %copy-start.3 = (bf16[64,1024]{1,0:T(8,128)(2,1)S(1)}, bf16[64,1024]{1,0:T(8,128)(2,1)}, u32[]{:S(2)}) copy-start(bf16[64,1024]{1,0:T(8,128)(2,1)} %get-tuple-element.15.value_ref) | copy-start | bytes 393220

commit v3 on v2

--- a/solution.py
+++ b/solution.py
@@ -453,30 +453,6 @@
         plan,
         1,
     )
-
-
-def turn(values, axis_kind, send_views, out_shapes, call_id, count, by_source=False):
-    def plan():
-        s, t = lax.axis_index("seq"), lax.axis_index("tp")
-        p, c = s // 2, lax.rem(s, 2)
-        rounds = []
-        for k in range(1, count):
-            if axis_kind == "tp":
-                me = t
-                peer = tp_peer
-            else:
-                me = p
-                peer = lambda i: {"seq": 2 * i + c}
-            target = lax.rem(me + k, count)
-            source = lax.rem(me + count - k, count)
-            items = [
-                (i, (lambda ref, v=view, to=target: v(ref, to)), i, slot(me if by_source else k - 1))
-                for i, view in enumerate(send_views)
-            ]
-            rounds.append((peer(source), peer(target), items))
-        return rounds
-
-    return exchange(values, out_shapes, plan, call_id)
 
 
 def blend_and_patch(attended, proj, byte_states, edge_states, bounds, used, lift, cross_kv, call_id):
@@ -686,13 +662,236 @@
     )(attended, proj, byte_states, edge_states, *bounds, used, lift, cross_kv)
 
 
-def swap_cores(value, call_id):
-    def plan():
-        s = lax.axis_index("seq")
-        other = seq_peer(s + 1 - 2 * lax.rem(s, 2))
-        return [(other, other, [(0, whole, 0, whole)])]
-
-    return exchange([value], [like(value.shape, value.dtype)], plan, call_id)[0]
+def latent_stage(rows, patches, used, gain, weights, projs, cosine, sine, query_pos, key_pos, call_id):
+    count = lax.axis_size("tp")
+    row_total, chip_width = rows.shape
+    half = chip_width // 2
+    slots, columns = patches.shape
+    full_width = columns * count
+
+    def kernel(
+        rows_ref, patch_ref, used_ref, gain_ref, cos_ref, sin_ref, qpos_ref, kpos_ref,
+        w_own_hbm, w_other_hbm, o_own_hbm, o_other_hbm,
+        out_ref,
+        w_own, w_other, o_own, o_other, geared, qkv_send, qkv_land, sq_send, sq_land,
+        kv_own, kv_other, att_all, parts, land, final,
+        load_sems, qkv_s, qkv_r, sq_s, sq_r, kv_sems, att_s, att_r, a_s, a_r, b_s, b_r,
+    ):
+        s, t = lax.axis_index("seq"), lax.axis_index("tp")
+        p, c = s // 2, lax.rem(s, 2)
+        pair_refs = ((w_own_hbm, w_own), (w_other_hbm, w_other), (o_own_hbm, o_own), (o_other_hbm, o_other))
+        loads = [
+            pltpu.make_async_copy(source, target, load_sems.at[i])
+            for i, (source, target) in enumerate(pair_refs)
+        ]
+        for load in loads:
+            load.start()
+
+        def plane(index):
+            return {"seq": 2 * index + c}
+
+        partner = seq_peer(s + 1 - 2 * c)
+        greet(
+            [plane(lax.rem(p + k, count)) for k in range(1, count)]
+            + [tp_peer(lax.rem(t + k, count)) for k in range(1, count)]
+            + [partner]
+        )
+
+        def send(source, target, send_sem, recv_sem, device):
+            return pltpu.make_async_remote_copy(
+                src_ref=source,
+                dst_ref=target,
+                send_sem=send_sem,
+                recv_sem=recv_sem,
+                device_id=device,
+                device_id_type=MESH,
+            )
+
+        values = rows_ref[...].astype(jnp.float32)
+        squares = jnp.sum(values * values, axis=1, keepdims=True)
+        eye = lax.broadcasted_iota(jnp.int32, (row_total, row_total), 0) == lax.broadcasted_iota(
+            jnp.int32, (row_total, row_total), 1
+        )
+        flat = jnp.sum(jnp.where(eye, squares, 0.0), axis=0, keepdims=True)
+        sq_send[...] = jnp.broadcast_to(flat, sq_send.shape)
+        geared[...] = (values * gain_ref[...]).astype(jnp.bfloat16)
+        sent = []
+        for k in range(1, count):
+            copy = send(
+                sq_send, sq_land.at[k - 1], sq_s.at[k - 1], sq_r.at[k - 1], plane(lax.rem(p + k, count))
+            )
+            copy.start()
+            sent.append(copy)
+        loads[0].wait()
+        loads[1].wait()
+        mine = geared[:, pl.ds(pl.multiple_of(c * half, half), half)]
+        theirs = geared[:, pl.ds(pl.multiple_of((1 - c) * half, half), half)]
+        total = []
+        for k in list(range(1, count)) + [0]:
+            target = lax.rem(p + k, count)
+            lanes = pl.ds(pl.multiple_of(target * HD, HD), HD)
+            for i in range(3):
+                part = jnp.dot(
+                    mine, w_own[i, :, lanes], preferred_element_type=jnp.float32
+                ) + jnp.dot(theirs, w_other[i, :, lanes], preferred_element_type=jnp.float32)
+                if k:
+                    qkv_send[k - 1, i] = part.astype(jnp.bfloat16)
+                else:
+                    total.append(part)
+            if k:
+                copy = send(
+                    qkv_send.at[k - 1], qkv_land.at[k - 1], qkv_s.at[k - 1], qkv_r.at[k - 1], plane(target)
+                )
+                copy.start()
+                sent.append(copy)
+        for copy in sent:
+            copy.wait_recv()
+        flat = flat + jnp.sum(sq_land[:, 0:1, :], axis=0)
+        square_sum = jnp.sum(jnp.where(eye, flat, 0.0), axis=1, keepdims=True)
+        scale = lax.rsqrt(square_sum / full_width + epsilon)
+        for i in range(3):
+            for k in range(count - 1):
+                total[i] = total[i] + qkv_land[k, i].astype(jnp.float32)
+            total[i] = total[i] * scale
+
+        def turned(vectors):
+            return (
+                vectors * cos_ref[...] + pltpu.roll(vectors, HD // 2, 1) * sin_ref[...]
+            ).astype(jnp.bfloat16)
+
+        queries = turned(total[0])
+        kv_own[0] = turned(total[1])
+        kv_own[1] = total[2].astype(jnp.bfloat16)
+        swap = send(kv_own, kv_other, kv_sems.at[0], kv_sems.at[1], partner)
+        swap.start()
+
+        def scored(keys, first):
+            scores = lax.dot_general(
+                queries, keys, (((1,), (1,)), ((), ())), preferred_element_type=jnp.float32
+            ) * (1.0 / math.sqrt(HD))
+            permitted = kpos_ref[:, first : first + row_total] <= qpos_ref[...]
+            return jnp.where(permitted, scores, -1e30), permitted
+
+        scores_a, permitted_a = scored(kv_own[0], 0)
+        swap.wait_recv()
+        scores_b, permitted_b = scored(kv_other[0], row_total)
+        largest = jnp.maximum(
+            jnp.max(scores_a, axis=1, keepdims=True), jnp.max(scores_b, axis=1, keepdims=True)
+        )
+        raised_a = jnp.where(permitted_a, jnp.exp(scores_a - largest), 0.0)
+        raised_b = jnp.where(permitted_b, jnp.exp(scores_b - largest), 0.0)
+        weight_sum = jnp.sum(raised_a, axis=1, keepdims=True) + jnp.sum(
+            raised_b, axis=1, keepdims=True
+        )
+        weighted = jnp.dot(
+            raised_a.astype(jnp.bfloat16), kv_own[1], preferred_element_type=jnp.float32
+        ) + jnp.dot(raised_b.astype(jnp.bfloat16), kv_other[1], preferred_element_type=jnp.float32)
+        att_all[p] = (weighted / weight_sum).astype(jnp.bfloat16)
+        heads = []
+        for k in range(1, count):
+            copy = send(
+                att_all.at[p], att_all.at[p], att_s.at[k - 1], att_r.at[p], plane(lax.rem(p + k, count))
+            )
+            copy.start()
+            heads.append(copy)
+        for k in range(1, count):
+            source = lax.rem(p + k, count)
+            send(
+                att_all.at[source], att_all.at[source], att_s.at[k - 1], att_r.at[source], plane(source)
+            ).wait_recv()
+        loads[2].wait()
+        loads[3].wait()
+        hops = []
+        for k in list(range(1, count)) + [0]:
+            target = lax.rem(p + k, count)
+            take = pl.ds(pl.multiple_of(target * slots, slots), slots)
+            attended = jnp.concatenate([att_all[j, take, :] for j in range(count)], axis=1)
+            for output, core in ((o_own, c), (o_other, 1 - c)):
+                parts[target, :, pl.ds(pl.multiple_of(core * half, half), half)] = jnp.dot(
+                    attended, output[...], preferred_element_type=jnp.float32
+                ).astype(jnp.bfloat16)
+            if k:
+                hop = send(
+                    parts.at[target], land.at[k - 1], a_s.at[k - 1], a_r.at[k - 1], plane(target)
+                )
+                hop.start()
+                hops.append(hop)
+        onward = []
+        for k in range(count):
+            origin = lax.rem(p + count - k, count)
+            if k == 0:
+                here = parts.at[p]
+            else:
+                hops[k - 1].wait_recv()
+                here = land.at[k - 1]
+            away = send(here, final.at[t], b_s.at[k], b_r.at[t], tp_peer(origin))
+            onward.append((origin, away))
+
+            @pl.when(origin != t)
+            def _():
+                away.start()
+
+            @pl.when(origin == t)
+            def _():
+                final[t] = here[...]
+
+        summed = patch_ref[...].astype(jnp.float32)
+        for q in range(count):
+
+            @pl.when(t != q)
+            def _():
+                send(land.at[0], final.at[q], b_s.at[q], b_r.at[q], tp_peer(t)).wait_recv()
+
+            summed = summed + final[q].astype(jnp.float32)
+        out_ref[...] = jnp.where(used_ref[...] > 0.0, summed, 0.0).astype(jnp.bfloat16)
+        for copy in sent + heads + hops + [swap]:
+            copy.wait_send()
+        for origin, away in onward:
+
+            @pl.when(origin != t)
+            def _():
+                away.wait_send()
+
+    vmem = pl.BlockSpec(memory_space=pltpu.VMEM)
+    hbm = pl.BlockSpec(memory_space=pl.ANY)
+    dma = pltpu.SemaphoreType.DMA
+    near = count - 1
+    return pl.pallas_call(
+        kernel,
+        out_shape=like((slots, columns)),
+        in_specs=[vmem] * 8 + [hbm] * 4,
+        out_specs=vmem,
+        scratch_shapes=[
+            pltpu.VMEM(weights[0].shape, jnp.bfloat16),
+            pltpu.VMEM(weights[1].shape, jnp.bfloat16),
+            pltpu.VMEM(projs[0].shape, jnp.bfloat16),
+            pltpu.VMEM(projs[1].shape, jnp.bfloat16),
+            pltpu.VMEM((row_total, chip_width), jnp.bfloat16),
+            pltpu.VMEM((near, 3, row_total, HD), jnp.bfloat16),
+            pltpu.VMEM((near, 3, row_total, HD), jnp.bfloat16),
+            pltpu.VMEM((8, row_total), jnp.float32),
+            pltpu.VMEM((near, 8, row_total), jnp.float32),
+            pltpu.VMEM((2, row_total, HD), jnp.bfloat16),
+            pltpu.VMEM((2, row_total, HD), jnp.bfloat16),
+            pltpu.VMEM((count, row_total, HD), jnp.bfloat16),
+            pltpu.VMEM((count, slots, columns), jnp.bfloat16),
+            pltpu.VMEM((near, slots, columns), jnp.bfloat16),
+            pltpu.VMEM((count, slots, columns), jnp.bfloat16),
+            dma((4,)),
+            dma((near,)),
+            dma((near,)),
+            dma((near,)),
+            dma((near,)),
+            dma((2,)),
+            dma((near,)),
+            dma((count,)),
+            dma((near,)),
+            dma((near,)),
+            dma((count,)),
+            dma((count,)),
+        ],
+        compiler_params=pltpu.CompilerParams(collective_id=call_id, has_side_effects=True),
+    )(rows, patches, used, gain, cosine, sine, query_pos, key_pos, *weights, *projs)
 
 
 def shards(
@@ -800,80 +999,32 @@
 
     rows = relay(patches, pairs, False, False, 4).reshape(pairs * slot_total, -1)
     half = rows.shape[1] // 2
-    full_width = half * size
-    values = rows.astype(jnp.float32)
-    squares = jnp.sum(values * values, axis=-1)
-    gain = lax.dynamic_slice_in_dim(latent_gain, p * 2 * half, 2 * half, 0)
-    geared = (values * gain.astype(jnp.float32)[None]).astype(jnp.bfloat16)
-    low, high = geared[:, :half], geared[:, half:]
-    partial = (
-        jnp.einsum(
-            "pd,idc->ipc", jnp.where(c == 0, low, high), lat_qkv, preferred_element_type=jnp.float32
-        )
-        + jnp.einsum(
-            "pd,idc->ipc",
-            jnp.where(c == 0, high, low),
-            lat_qkv_other,
-            preferred_element_type=jnp.float32,
-        )
-    ).astype(jnp.bfloat16)
-    row_total = rows.shape[0]
-    square_block = jnp.pad(
-        squares.reshape(row_total // 128, 128), ((0, 8 - row_total // 128), (0, 0))
-    )
-    parts, square_parts = turn(
-        [partial, square_block],
-        "pair",
-        [lambda ref, target: ref.at[:, :, pl.ds(pl.multiple_of(target * HD, HD), HD)], lambda ref, target: ref],
-        [like((pairs - 1, 3, row_total, HD)), like((pairs - 1, 8, 128), jnp.float32)],
-        5,
-        pairs,
-    )
-    projected = lax.dynamic_slice_in_dim(partial, p * HD, HD, 2).astype(jnp.float32) + jnp.sum(
-        parts.astype(jnp.float32), axis=0
-    )
-    square_sum = (square_block + jnp.sum(square_parts, axis=0)).reshape(-1)[:row_total]
-    projected = projected * lax.rsqrt(square_sum / full_width + epsilon)[None, :, None]
-    queries = rotate(projected[0][:, None], position)[:, 0].astype(jnp.bfloat16)
-    keys = rotate(projected[1][:, None], position)[:, 0].astype(jnp.bfloat16)
-    key_value = jnp.stack([keys, projected[2].astype(jnp.bfloat16)])
-    key_value_other = swap_cores(key_value, 6)
-    all_keys = jnp.concatenate([key_value[0], key_value_other[0]], axis=0)
-    all_values = jnp.concatenate([key_value[1], key_value_other[1]], axis=0)
+    gain = lax.dynamic_slice_in_dim(latent_gain, p * 2 * half, 2 * half, 0).astype(jnp.float32)
+    frequency = jnp.power(
+        rope_base, -2.0 * jnp.arange(HD // 2, dtype=jnp.float32) / HD
+    )
+    angles = position.astype(jnp.float32)[:, None] * frequency[None, :]
+    sine = jnp.sin(angles)
+    cosine = jnp.cos(angles)
     key_position = jnp.concatenate(
         [
             jnp.where(rows_used, position, far_position),
             jnp.where(other_used, other_position, far_position),
         ]
     )
-    scores = jnp.dot(queries, all_keys.T, preferred_element_type=jnp.float32) * (
-        1.0 / math.sqrt(HD)
-    )
-    permitted = key_position[None, :] <= position[:, None]
-    weights = masked_softmax(scores, permitted).astype(jnp.bfloat16)
-    attended = jnp.dot(weights, all_values, preferred_element_type=jnp.float32).astype(
-        jnp.bfloat16
-    )
-    (heads,) = turn(
-        [attended],
-        "pair",
-        [lambda ref, target: ref],
-        [like((pairs, row_total, HD))],
-        7,
-        pairs,
-        by_source=True,
-    )
-    attended = jnp.concatenate(
-        [jnp.where(p == q, attended, heads[q]) for q in range(pairs)], axis=1
-    )
-    own_out = jnp.dot(attended, lat_proj_out, preferred_element_type=jnp.float32)
-    other_out = jnp.dot(attended, lat_proj_other, preferred_element_type=jnp.float32)
-    partials = jnp.concatenate(
-        [jnp.where(c == 0, own_out, other_out), jnp.where(c == 0, other_out, own_out)], axis=1
-    ).astype(jnp.bfloat16)
-    reduced = relay(partials.reshape(pairs, slot_total, -1), pairs, True, True, 8)
-    latent = patches.astype(jnp.float32) + jnp.sum(reduced.astype(jnp.float32), axis=0)
-    latent = jnp.where(in_use[:, None], latent, 0.0).astype(jnp.bfloat16)
+    latent = latent_stage(
+        rows,
+        patches,
+        used_rows,
+        gain[None],
+        (lat_qkv, lat_qkv_other),
+        (lat_proj_out, lat_proj_other),
+        jnp.concatenate([cosine, cosine], axis=1),
+        jnp.concatenate([-sine, sine], axis=1),
+        position[:, None],
+        key_position[None, :],
+        5,
+    )
     return (encoded, latent)
 
 

time: 152 us -> 156 us (1.026)
  local copies, waits for them, and re-layouts: 9 us -> 22.9 us
  matrix products: 9.66 us -> 4.16 us
  other arithmetic: 20.8 us -> 16 us
    pallas_call x0 -> x1, Pallas kernels: none -> 41.7 us  [latent_stage(): pl.pallas_call(kernel, out_shape=like((slots, columns)), in_specs=[vmem]...]
    pallas_call x2 -> x1, Pallas kernels: 37.3 us -> 15.1 us  [relay(): pl.pallas_call(kernel, out_shape=jax.ShapeDtypeStruct((count, *block), va...]
    pallas_call x4 -> x1, Pallas kernels: 33.7 us -> 13.9 us  [exchange(): pl.pallas_call(kernel, out_shape=out_shapes, in_specs=[pl.BlockSpec(memor...]
    dot_general x6 -> x0, matrix products: 6.43 us -> none  [the longest x1 2.88 us: shards(): jnp.einsum('pd,idc->ipc', jnp.where(c == 0, high, low), lat_qkv_other, pr...]
    reduce_sum x6 -> x1, other arithmetic: 4.76 us -> 0.22 us  [slots_of(): used = jnp.sum(jnp.where(hit, count_list[None, :], 0), axis=1)]
    slice x3, local copies, waits for them, and re-layouts: 1.33 us -> 5.16 us  [shards(): behind[k, 1]]
    convert_element_type x6 -> x0, other arithmetic: 2.76 us -> none  [the longest x2 1.83 us: shards(): geared = (values * gain.astype(jnp.float32)[None]).astype(jnp.bfloat16)]
    unnamed x12 -> x31, local copies, waits for them, and re-layouts: 0.04 us -> 2.79 us
  transfers between devices with their start and end apart: 2 -> 2, of which waited for: 0 -> 0; matrix products, arithmetic and copies ran while one was open for 23% -> 26% of each run, Pallas kernels for 57% -> 43%
where the time goes in v3:
time: 156 us; the launch traced here: 154 us
  Pallas kernels  108 us (69%)
  local copies, waits for them, and re-layouts  22.9 us (15%)
  other arithmetic  16 us (10%)
  matrix products  4.16 us (3%)
  between operations  2.25 us (1%)
    pallas_call x1, Pallas kernels, latent_stage(): pl.pallas_call(kernel, out_shape=like((slots, columns)), in_specs=[vmem]...  41.7 us
    pallas_call x1, Pallas kernels, blend_and_patch(): pl.pallas_call(kernel, out_shape=[like((total_rows, width)), like((slots,...  37.6 us
    pallas_call x1, Pallas kernels, relay(): pl.pallas_call(kernel, out_shape=jax.ShapeDtypeStruct((count, *block), va...  15.1 us
    pallas_call x1, Pallas kernels, exchange(): pl.pallas_call(kernel, out_shape=out_shapes, in_specs=[pl.BlockSpec(memor...  13.9 us
    slice x3, local copies, waits for them, and re-layouts, shards(): behind[k, 1]  5.16 us
  transfers between devices with their start and end apart: 2, of which 0 were waited for; matrix products, arithmetic and copies ran while one was open for 26% of the time, Pallas kernels for 43%

profile of v3, /device:TPU:6, one launch (start us, length us, event | category | flops | bytes accessed | tf_op | source)
XLA Modules:
  0.0 154.2 jit_solution(15622172936954211797)
XLA Ops:
  0.7 0.5 collective-permute-start.1
  1.2 0.6 iota_add_fusion.2
  1.8 0.6 iota_add_fusion
  2.4 0.6 broadcast_compare_fusion
  3.0 1.3 slice_bitcast_fusion
  4.3 1.2 subtract_bitcast_fusion
  5.5 0.5 compare_select_fusion
  6.0 0.7 convert_element_type.46
  6.7 1.2 fusion.8
  8.0 0.7 compare_select_fusion.2
  9.3 1.7 %fusion.6.refs_0_ = bf16[3,256,256]{2,1,0:T(8,128)(2,1)S(1)} fusion(bf16[3,1024,256]{2,1,0:T(8,128)(2,1)S(1)} %copy-done, bf16[256,1024]{1,0:T(8,128)(2,1)} %states_ref.1, f32[1024]{0:T(1024)S(1)} %convert_element_type.46, f32[256]{0:T(256)S(1)} %add_rsqrt_fusion), kind=kOutput, calls=%fused_computation.12 | convolution fusion | flops 403898368 | bytes 2495488 | tf_op jit(solution)/shard_map/bd,idc->ibc/dot_general | solution.py:921
  11.0 0.8 fusion.47
  11.8 0.6 broadcast_select_fusion.1.refs_2_
  12.4 13.9 %shard_map.122 = (bf16[2,2,256,256]{3,2,1,0:T(8,128)(2,1)}, bf16[3,16,256]{2,1,0:T(8,128)(2,1)}, bf16[16,1024]{1,0:T(8,128)(2,1)}, s32[7,8,128]{2,1,0:T(8,128)}) custom-call(bf16[3,256,256]{2,1,0:T(8,128)(2,1)} %copy-done.1, bf16[256,1024]{1,0:T(8,128)(2,1)} %states_ref.1, s32[8,128]{1,0:T(8,128)} %broadcast_select_fusion.1.refs_2_), custom_call_target="tpu_custom_call" | custom-call | tf_op jit(solution)/shard_map/pallas_call | solution.py:292
  26.3 0.7 fusion.48
  27.0 0.7 copy.80
  27.8 1.0 copy.70
  28.8 1.8 %fusion.46 = (bf16[1,1,256,256]{3,2,1,0:T(8,128)(2,1)}, bf16[1,1,256,256]{3,2,1,0:T(8,128)(2,1)S(1)}, bf16[1,1,256,256]{3,2,1,0:T(8,128)(2,1)}, bf16[1,1,256,256]{3,2,1,0:T(8,128)(2,1)}) fusion(bf16[2,2,256,256]{3,2,1,0:T(8,128)(2,1)} %get-tuple-element.8), kind=kLoop, calls=%fused_computation.92 | loop fusion | bytes 1048576 | tf_op jit(solution)/shard_map/slice | solution.py:934
  30.7 1.0 copy.68
  31.7 0.7 copy.79
  32.4 1.6 %copy.66 = bf16[1,256,256]{1,2,0:T(8,128)(2,1)} copy(bf16[1,256,256]{2,1,0:T(8,128)(2,1)} %get-tuple-element.24) | data formatting | bytes 262144 | tf_op jit(solution)/shard_map/slice | solution.py:936
  34.1 0.7 copy.78
  34.8 1.7 %copy.64 = bf16[1,256,256]{1,2,0:T(8,128)(2,1)} copy(bf16[1,256,256]{2,1,0:T(8,128)(2,1)} %get-tuple-element.22) | data formatting | bytes 262144 | tf_op jit(solution)/shard_map/slice | solution.py:934
  36.5 1.7 %copy.63 = bf16[1,1,256,256]{2,3,1,0:T(8,128)(2,1)} copy(bf16[1,1,256,256]{3,2,1,0:T(8,128)(2,1)} %get-tuple-element.21) | data formatting | bytes 262144 | tf_op jit(solution)/shard_map/slice | solution.py:934
  38.1 1.7 %copy.62 = bf16[1,1,256,256]{2,3,1,0:T(8,128)(2,1)} copy(bf16[1,1,256,256]{3,2,1,0:T(8,128)(2,1)} %get-tuple-element.18) | data formatting | bytes 262144 | tf_op jit(solution)/shard_map/slice | solution.py:934
  39.8 1.0 and_and_fusion
  40.8 1.6 %fusion.22 = f32[4,272,784]{2,1,0:T(8,128)S(1)} fusion(bf16[16,4,64]{0,2,1:T(8,128)(2,1)} %bitcast.39, bf16[256,4,64]{0,2,1:T(8,128)(2,1)S(1)} %bitcast.35, bf16[256,4,64]{0,2,1:T(8,128)(2,1)S(1)} %bitcast.36, bf16[256,4,64]{0,2,1:T(8,128)(2,1)S(1)} %bitcast.37, bf16[16,4,64]{0,2,1:T(8,128)(2,1)} %bitcast.40, bf16[256,4,64]{0,2,1:T(8,128)(2,1)} %bitcast.38), kind=kOutput, calls=%fused_computation.28 | convolution fusion | flops 111067136 | bytes 3952640 | tf_op jit(solution)/shard_map/qhd,khd->hqk/dot_general | solution.py:939
  42.5 2.3 %fusion.49 = (f32[4,272]{1,0:T(4,128)S(1)}, f32[4,272,784]{2,1,0:T(8,128)S(1)}) fusion(f32[4,272,784]{2,1,0:T(8,128)S(1)} %fusion.22, pred[272,784]{1,0:T(8,128)(4,1)S(1)} %and_and_fusion), kind=kOutput, calls=%fused_computation.95 | output fusion | flops 5971727 | bytes 7041536 | tf_op jit(solution)/shard_map/sub | solution.py:55
  44.8 0.8 fusion.7
  45.7 0.8 copy.74.att_ref
  46.6 0.6 slice.59
  47.3 0.6 fusion.34.used_ref
  48.5 0.6 subtract_select_fusion
  49.2 37.6 %shard_map.123 = (bf16[272,1024]{1,0:T(8,128)(2,1)}, bf16[64,1024]{1,0:T(8,128)(2,1)}) custom-call(bf16[272,256]{1,0:T(8,128)(2,1)} %copy.74.att_ref, bf16[256,1024]{1,0:T(8,128)(2,1)} %proj_ref.1, bf16[256,1024]{1,0:T(8,128)(2,1)} %states_ref.1, bf16[16,1024]{1,0:T(8,128)(2,1)} %get-tuple-element.10.edge_ref, s32[64,1]{1,0:T(8,128)} %get-tuple-element.37.lo_ref, ...), custom_call_target="tpu_custom_call" | custom-call | tf_op jit(solution)/shard_map/pallas_call | solution.py:638
  86.8 1.9 %slice.60 = bf16[256,1024]{1,0:T(8,128)(2,1)} slice(bf16[272,1024]{1,0:T(8,128)(2,1)} %get-tuple-element.12), slice={[0:256], [0:1024]} | slice | bytes 1048576 | tf_op jit(solution)/shard_map/slice | solution.py:987
  88.7 15.1 %shard_map.124 = bf16[4,64,1024]{2,1,0:T(8,128)(2,1)} custom-call(bf16[64,1024]{1,0:T(8,128)(2,1)} %get-tuple-element.13.value_ref.patch_ref), custom_call_target="tpu_custom_call" | custom-call | tf_op jit(solution)/shard_map/pallas_call | solution.py:403
  103.9 0.2 fusion.36
  104.3 0.1 select_reduce_fusion
  104.4 0.2 select_reduce_fusion.4
  104.8 0.8 add.162.qpos_ref
  105.7 0.6 pad_add_fusion.1
  106.3 1.3 dynamic-slice_convert_fusion
  107.6 0.5 fusion.33
  108.2 0.8 pad_maximum_fusion.cos_ref
  108.9 0.8 pad_maximum_fusion.1.sin_ref
  109.7 1.2 copy-done.2
  110.8 41.7 %shard_map.125 = bf16[64,1024]{1,0:T(8,128)(2,1)} custom-call(bf16[256,1024]{1,0:T(8,128)(2,1)} %bitcast.34, bf16[64,1024]{1,0:T(8,128)(2,1)} %get-tuple-element.13.value_ref.patch_ref, f32[64,1]{1,0:T(8,128)} %fusion.34.used_ref, f32[1,1024]{1,0:T(1,128)} %bitcast.46, f32[256,128]{1,0:T(8,128)} %pad_maximum_fusion.cos_ref, ...), custom_call_target="tpu_custom_call" | custom-call | tf_op jit(solution)/shard_map/pallas_call | solution.py:859
  152.6 1.6 %copy.83 = bf16[64,1024]{1,0:T(8,128)(2,1)} copy(bf16[64,1024]{1,0:T(8,128)(2,1)} %shard_map.125) | data formatting | bytes 262144
  (47 shorter events, 1.0 us)
Async XLA Ops:
  0.6 8.6 %copy-start = (bf16[3,1024,256]{2,1,0:T(8,128)(2,1)S(1)}, bf16[3,1024,256]{2,1,0:T(8,128)(2,1)}, u32[]{:S(2)}) copy-start(bf16[3,1024,256]{2,1,0:T(8,128)(2,1)} %param.13) | copy-start | bytes 4718596
  0.6 109.0 %collective-permute-start = (bf16[3,512,512]{2,1,0:T(8,128)(2,1)}, bf16[3,512,512]{2,1,0:T(8,128)(2,1)S(1)}, u32[]{:S(2)}, u32[]{:S(2)}) collective-permute-start(bf16[3,512,512]{2,1,0:T(8,128)(2,1)} %w_own_hbm.1), channel_id=1, source_target_pairs={{0,4},{4,0},{8,12},{12,8},{16,20},{20,16},{24,28},{28,24},{1,5},{5... | collective-permute-start | bytes 4718600 | tf_op jit(solution)/shard_map/ppermute | solution.py:917
  0.7 109.0 %collective-permute-start.1 = (bf16[512,512]{1,0:T(8,128)(2,1)}, bf16[512,512]{1,0:T(8,128)(2,1)}, u32[]{:S(2)}, u32[]{:S(2)}) collective-permute-start(bf16[512,512]{1,0:T(8,128)(2,1)} %o_own_hbm.1), channel_id=1, source_target_pairs={{0,4},{4,0},{8,12},{12,8},{16,20},{20,16},{24,28},{28,24},{1,5},{5... | collective-permute-start | bytes 1572872 | tf_op jit(solution)/shard_map/ppermute | solution.py:918
  1.2 25.1 %copy-start.8 = (pred[128]{0:T(512)(128)(4,1)}, pred[128]{0:T(512)(128)(4,1)S(1)}, u32[]{:S(2)}) copy-start(pred[128]{0:T(512)(128)(4,1)S(1)} %iota_compare_fusion.7) | copy-start | bytes 388
  8.6 3.2 %copy-start.10 = (s32[128]{0:T(128)}, s32[128]{0:T(128)S(1)}, u32[]{:S(2)}) copy-start(s32[128]{0:T(128)S(1)} %compare_select_fusion.2) | copy-start | bytes 1540
  11.0 1.5 copy-start.1
  42.4 2.3 %copy-start.3 = (bf16[1,256,256]{1,2,0:T(8,128)(2,1)S(1)}, bf16[1,256,256]{1,2,0:T(8,128)(2,1)}, u32[]{:S(2)}) copy-start(bf16[1,256,256]{1,2,0:T(8,128)(2,1)} %copy.64) | copy-start | bytes 393220
  42.4 2.3 %copy-start.4 = (bf16[1,1,256,256]{2,3,1,0:T(8,128)(2,1)S(1)}, bf16[1,1,256,256]{2,3,1,0:T(8,128)(2,1)}, u32[]{:S(2)}) copy-start(bf16[1,1,256,256]{2,3,1,0:T(8,128)(2,1)} %copy.63) | copy-start | bytes 393220
  42.4 2.3 %copy-start.5 = (bf16[1,1,256,256]{2,3,1,0:T(8,128)(2,1)S(1)}, bf16[1,1,256,256]{2,3,1,0:T(8,128)(2,1)}, u32[]{:S(2)}) copy-start(bf16[1,1,256,256]{2,3,1,0:T(8,128)(2,1)} %copy.62) | copy-start | bytes 393220
  42.5 2.3 %copy-start.6 = (bf16[1,16,256]{1,2,0:T(8,128)(2,1)S(1)}, bf16[1,16,256]{1,2,0:T(8,128)(2,1)}, u32[]{:S(2)}) copy-start(bf16[1,16,256]{1,2,0:T(8,128)(2,1)} %copy.78) | copy-start | bytes 24580
  44.8 1.7 %copy-start.14 = (s32[63,1]{0,1:T(1,128)S(1)}, s32[63,1]{0,1:T(1,128)}, u32[]{:S(2)}) copy-start(s32[63,1]{0,1:T(1,128)} %slice_bitcast_fusion) | copy-start | bytes 760
  44.8 1.8 %copy-start.7 = (s32[7,8,128]{2,1,0:T(8,128)S(1)}, s32[7,8,128]{2,1,0:T(8,128)}, u32[]{:S(2)}) copy-start(s32[7,8,128]{2,1,0:T(8,128)} %get-tuple-element.11) | copy-start | bytes 86020
  44.8 2.4 %copy-start.12 = (s32[64,1]{0,1:T(1,128)S(1)}, s32[64,1]{0,1:T(1,128)}, u32[]{:S(2)}) copy-start(s32[64,1]{0,1:T(1,128)} %subtract_bitcast_fusion) | copy-start | bytes 772
  49.2 54.7 %copy-start.9 = (pred[128]{0:T(512)(128)(4,1)S(1)}, pred[128]{0:T(512)(128)(4,1)}, u32[]{:S(2)}) copy-start(pred[128]{0:T(512)(128)(4,1)} %copy-done.8) | copy-start | bytes 388
  49.2 54.7 %copy-start.11 = (s32[128]{0:T(128)S(1)}, s32[128]{0:T(128)}, u32[]{:S(2)}) copy-start(s32[128]{0:T(128)} %copy-done.10) | copy-start | bytes 1540
  49.2 55.0 %copy-start.13 = (s32[8]{0:T(128)S(1)}, s32[8]{0:T(128)}, u32[]{:S(2)}) copy-start(s32[8]{0:T(128)} %compare_select_fusion) | copy-start | bytes 100
  109.7 1.2 copy-start.2

commit v4 on v3

--- a/solution.py
+++ b/solution.py
@@ -455,7 +455,9 @@
     )
 
 
-def blend_and_patch(attended, proj, byte_states, edge_states, bounds, used, lift, cross_kv, call_id):
+def encode_and_patch(
+    projected, behind, edge, proj, byte_states, edge_states, bounds, used, lift, cross_kv, call_id
+):
     count = lax.axis_size("tp")
     byte_rows, width = byte_states.shape
     share = byte_rows // count
@@ -464,11 +466,13 @@
     slots = bounds[0].shape[0]
     columns = lift.shape[1]
     total_rows = byte_rows + EDGE
+    reach = behind.shape[0]
 
     def kernel(
-        att_ref, proj_ref, states_ref, edge_ref, lo_ref, hi_ref, used_ref, lift_hbm, cross_hbm,
-        full_ref, patch_ref,
-        sends, lands, tail_send, tail_land, blocks, lift_ref, cross_ref, pooled_ref,
+        own_ref, behind_ref, next_ref, proj_ref, states_ref, edge_ref, lo_ref, hi_ref, used_ref,
+        lift_hbm, cross_hbm,
+        enc_ref, patch_ref,
+        sends, lands, tail_send, tail_land, blocks, lift_ref, cross_ref, pooled_ref, full_ref,
         load_sems, rs_send, rs_recv, tail_s, tail_r, up_send, down_send, ag_recv,
     ):
         t = lax.axis_index("tp")
@@ -478,9 +482,38 @@
         ]
         for load in loads:
             load.start()
-        blend = jnp.dot(att_ref[...], proj_ref[...], preferred_element_type=jnp.float32).astype(
-            jnp.bfloat16
+        key_rows, value_rows = (
+            jnp.concatenate(
+                [behind_ref[k, i] for k in range(reach - 1, -1, -1)]
+                + [own_ref[i + 1], next_ref[i + 1]],
+                axis=0,
+            )
+            for i in range(2)
         )
+        query_rows = jnp.concatenate([own_ref[0], next_ref[0]], axis=0)
+        reach_shape = (total_rows, WIN + total_rows)
+        query_at = lax.broadcasted_iota(jnp.int32, reach_shape, 0)
+        key_at = lax.broadcasted_iota(jnp.int32, reach_shape, 1) - WIN
+        near = (
+            (key_at <= query_at)
+            & (key_at > query_at - WIN)
+            & (key_at >= -lax.axis_index("seq") * byte_rows)
+        )
+        head_of = lax.broadcasted_iota(jnp.int32, query_rows.shape, 1) // EH
+        attended = jnp.zeros(query_rows.shape, jnp.float32)
+        for head in range(query_rows.shape[1] // EH):
+            scores = lax.dot_general(
+                jnp.where(head_of == head, query_rows, jnp.zeros_like(query_rows)),
+                key_rows,
+                (((1,), (1,)), ((), ())),
+                preferred_element_type=jnp.float32,
+            ) * (1.0 / math.sqrt(EH))
+            weights = masked_softmax(scores, near).astype(jnp.bfloat16)
+            seen = jnp.dot(weights, value_rows, preferred_element_type=jnp.float32)
+            attended = jnp.where(head_of == head, seen, attended)
+        blend = jnp.dot(
+            attended.astype(jnp.bfloat16), proj_ref[...], preferred_element_type=jnp.float32
+        ).astype(jnp.bfloat16)
         for q in range(count):
             for h in range(chunks):
                 begin = q * share + h * piece
@@ -572,6 +605,7 @@
             for h in range(chunks):
                 begin = q * share + h * piece
                 full_ref[begin : begin + piece] = blocks[q, h]
+                enc_ref[begin : begin + piece] = blocks[q, h]
         for load in loads:
             load.wait()
 
@@ -637,8 +671,8 @@
     dma = pltpu.SemaphoreType.DMA
     return pl.pallas_call(
         kernel,
-        out_shape=[like((total_rows, width)), like((slots, columns))],
-        in_specs=[vmem] * 7 + [hbm] * 2,
+        out_shape=[like((byte_rows, width)), like((slots, columns))],
+        in_specs=[vmem] * 9 + [hbm] * 2,
         out_specs=[vmem, vmem],
         scratch_shapes=[
             pltpu.VMEM((count, chunks, piece, width), jnp.bfloat16),
@@ -649,6 +683,7 @@
             pltpu.VMEM(lift.shape, lift.dtype),
             pltpu.VMEM(cross_kv.shape, cross_kv.dtype),
             pltpu.VMEM((slots, width), jnp.bfloat16),
+            pltpu.VMEM((total_rows, width), jnp.bfloat16),
             dma((2,)),
             dma((chunks, count - 1)),
             dma((chunks, count - 1)),
@@ -659,7 +694,7 @@
             dma((count, chunks)),
         ],
         compiler_params=pltpu.CompilerParams(collective_id=call_id, has_side_effects=True),
-    )(attended, proj, byte_states, edge_states, *bounds, used, lift, cross_kv)
+    )(projected, behind, edge, proj, byte_states, edge_states, *bounds, used, lift, cross_kv)
 
 
 def latent_stage(rows, patches, used, gain, weights, projs, cosine, sine, query_pos, key_pos, call_id):
@@ -926,37 +961,6 @@
     lanes = lax.broadcasted_iota(jnp.int32, (8, 128), 1)
     info = jnp.where(lanes == 0, patch_count, jnp.where(lanes == 1, local_starts[0], 0))
     behind, edge, edge_states, infos = halo(projected, byte_states, info)
-    reach = WIN // byte_rows
-    key_rows = jnp.concatenate(
-        [behind[k, 0] for k in range(reach - 1, -1, -1)] + [projected[1], edge[1]], axis=0
-    )
-    value_rows = jnp.concatenate(
-        [behind[k, 1] for k in range(reach - 1, -1, -1)] + [projected[2], edge[2]], axis=0
-    )
-    query_rows = jnp.concatenate([projected[0], edge[0]], axis=0)
-    total_rows = byte_rows + EDGE
-    head_count = projected.shape[2] // EH
-    scores = jnp.einsum(
-        "qhd,khd->hqk",
-        query_rows.reshape(total_rows, head_count, EH),
-        key_rows.reshape(-1, head_count, EH),
-        preferred_element_type=jnp.float32,
-    ) * (1.0 / math.sqrt(EH))
-    query_pos = anchor + jnp.arange(total_rows, dtype=jnp.int32)
-    key_pos = anchor - WIN + jnp.arange(WIN + total_rows, dtype=jnp.int32)
-    allowed = (
-        (key_pos[None, :] <= query_pos[:, None])
-        & (key_pos[None, :] > query_pos[:, None] - WIN)
-        & (key_pos[None, :] >= 0)
-    )
-    weights = masked_softmax(scores, allowed[None]).astype(jnp.bfloat16)
-    attended = jnp.einsum(
-        "hqk,khd->qhd",
-        weights,
-        value_rows.reshape(-1, head_count, EH),
-        preferred_element_type=jnp.float32,
-    )
-    attended = attended.reshape(total_rows, head_count * EH).astype(jnp.bfloat16)
     recent = jnp.concatenate([info[None], infos], axis=0)
     ring = jnp.arange(size, dtype=jnp.int32)
     from_ring = lax.rem(s - ring + size, size)
@@ -973,8 +977,10 @@
     lower = jnp.where(in_use, local_starts - anchor, 0)[:, None]
     upper = jnp.where(in_use, patch_end - anchor, 1)[:, None]
     used_rows = in_use.astype(jnp.float32)[:, None]
-    extended, patches = blend_and_patch(
-        attended,
+    encoded, patches = encode_and_patch(
+        projected,
+        behind,
+        edge,
         enc_proj_out,
         byte_states,
         edge_states,
@@ -984,7 +990,6 @@
         cross_kv,
         2,
     )
-    encoded = extended[:byte_rows]
 
     def slots_of(core):
         members = 2 * jnp.arange(pairs, dtype=jnp.int32) + core

time: 156 us -> 135 us (0.87)
  local copies, waits for them, and re-layouts: 22.9 us -> 7.83 us
  other arithmetic: 16 us -> 10.6 us
  Pallas kernels: 108 us -> 111 us
  matrix products: 4.16 us -> 2.41 us
    slice x11 -> x0, local copies, waits for them, and re-layouts: 14 us -> none  [the longest x3 5.16 us: shards(): behind[k, 1]]
    dot_general x2 -> x0, matrix products: 2.49 us -> none  [the longest x1 1.65 us: shards(): jnp.einsum('qhd,khd->hqk', query_rows.reshape(total_rows, head_count, EH)...]
    sub x1 -> x0, other arithmetic: 2.28 us -> none  [masked_softmax(): raised = jnp.where(allowed, jnp.exp(scores - largest), 0.0)]
    concatenate x3 -> x0, local copies, waits for them, and re-layouts: 2.17 us -> none  [the longest x1 0.73 us: shards(): jnp.concatenate([behind[k, 0] for k in range(reach - 1, -1, -1)] + [proje...]
    pallas_call x1, Pallas kernels: 37.6 us -> 39.8 us  [encode_and_patch(): pl.pallas_call(kernel, out_shape=[like((byte_rows, width)), like((slots,...]
    unnamed x31 -> x6, local copies, waits for them, and re-layouts: 2.79 us -> 4.6 us
  transfers between devices with their start and end apart: 2 -> 2, of which waited for: 0 -> 0; matrix products, arithmetic and copies ran while one was open for 26% -> 12% of each run, Pallas kernels for 43% -> 51%
where the time goes in v4:
time: 135 us; the launch traced here: 134 us
  Pallas kernels  111 us (82%)
  other arithmetic  10.6 us (8%)
  local copies, waits for them, and re-layouts  7.83 us (6%)
  matrix products  2.41 us (2%)
  between operations  2.05 us (2%)
    pallas_call x1, Pallas kernels, latent_stage(): pl.pallas_call(kernel, out_shape=like((slots, columns)), in_specs=[vmem]...  41.7 us
    pallas_call x1, Pallas kernels, encode_and_patch(): pl.pallas_call(kernel, out_shape=[like((byte_rows, width)), like((slots,...  39.8 us
    pallas_call x1, Pallas kernels, relay(): pl.pallas_call(kernel, out_shape=jax.ShapeDtypeStruct((count, *block), va...  15.1 us
    pallas_call x1, Pallas kernels, exchange(): pl.pallas_call(kernel, out_shape=out_shapes, in_specs=[pl.BlockSpec(memor...  13.9 us
    unnamed x6, local copies, waits for them, and re-layouts  4.6 us
  transfers between devices with their start and end apart: 2, of which 0 were waited for; matrix products, arithmetic and copies ran while one was open for 12% of the time, Pallas kernels for 51%

profile of v4, /device:TPU:6, one launch (start us, length us, event | category | flops | bytes accessed | tf_op | source)
XLA Modules:
  0.0 134.0 jit_solution(12586077368822971372)
XLA Ops:
  0.6 0.0 copy-start
  0.6 0.1 collective-permute-start.1
  0.7 0.5 collective-permute-start
  1.9 0.7 slice_bitcast_fusion
  2.6 0.6 compare_select_fusion.2
  3.3 0.7 subtract_bitcast_fusion
  3.9 1.2 fusion.1
  5.2 0.6 broadcast_select_fusion.1.refs_2_
  5.8 0.7 convert_element_type.36
  6.5 0.1 copy.21
  6.6 0.1 pad_add_fusion.2
  6.6 0.1 copy.22
  6.7 0.6 fusion.9.used_ref
  7.3 0.0 copy-done
  7.3 2.4 %fusion.refs_0_.own_ref = bf16[3,256,256]{2,1,0:T(8,128)(2,1)} fusion(bf16[3,1024,256]{2,1,0:T(8,128)(2,1)S(1)} %copy-done, bf16[256,1024]{1,0:T(8,128)(2,1)} %states_ref.1, f32[1024]{0:T(1024)S(1)} %convert_element_type.36, f32[256]{0:T(256)S(1)} %add_rsqrt_fusion), kind=kOutput, calls=%fused_computation.3 | convolution fusion | flops 403898368 | bytes 2495488 | tf_op jit(solution)/shard_map/bd,idc->ibc/dot_general | solution.py:956
  9.7 13.9 %shard_map.122 = (bf16[2,2,256,256]{3,2,1,0:T(8,128)(2,1)}, bf16[3,16,256]{2,1,0:T(8,128)(2,1)}, bf16[16,1024]{1,0:T(8,128)(2,1)}, s32[7,8,128]{2,1,0:T(8,128)}) custom-call(bf16[3,256,256]{2,1,0:T(8,128)(2,1)} %fusion.refs_0_.own_ref, bf16[256,1024]{1,0:T(8,128)(2,1)} %states_ref.1, s32[8,128]{1,0:T(8,128)} %broadcast_select_fusion.1.refs_2_), custom_call_target="tpu_custom_call" | custom-call | tf_op jit(solution)/shard_map/pallas_call | solution.py:292
  23.6 1.3 slice.16
  24.9 1.0 fusion.11
  26.5 0.6 subtract_select_fusion
  27.2 39.8 %shard_map.123 = (bf16[256,1024]{1,0:T(8,128)(2,1)}, bf16[64,1024]{1,0:T(8,128)(2,1)}) custom-call(bf16[3,256,256]{2,1,0:T(8,128)(2,1)} %fusion.refs_0_.own_ref, bf16[2,2,256,256]{3,2,1,0:T(8,128)(2,1)} %get-tuple-element.8.behind_ref, bf16[3,16,256]{2,1,0:T(8,128)(2,1)} %get-tuple-element.9.next_ref, bf16[256,1024]{1,0:T(8,128)(2,1)} %proj_ref.1, ...), custom_call_target="tpu_custom_call" | custom-call | tf_op jit(solution)/shard_map/pallas_call | solution.py:672
  67.0 0.1 select_reduce_fusion.1
  67.1 0.1 select_reduce_fusion
  67.2 0.2 select_reduce_fusion.4
  67.4 0.1 fusion.12
  67.5 0.1 select_n.102
  67.6 0.1 convert_element_type.42
  67.7 0.1 select_n.106
  67.8 0.8 add.125.qpos_ref
  68.6 15.1 %shard_map.124 = bf16[4,64,1024]{2,1,0:T(8,128)(2,1)} custom-call(bf16[64,1024]{1,0:T(8,128)(2,1)} %get-tuple-element.13.value_ref.patch_ref), custom_call_target="tpu_custom_call" | custom-call | tf_op jit(solution)/shard_map/pallas_call | solution.py:403
  83.7 0.6 pad_add_fusion.1
  84.3 1.3 dynamic-slice_convert_fusion
  85.6 0.5 fusion.8
  86.1 0.8 pad_maximum_fusion.cos_ref
  86.9 0.8 pad_maximum_fusion.1.sin_ref
  87.7 0.0 collective-permute-done.1.o_other_hbm
  87.7 0.0 collective-permute-done.w_other_hbm
  87.7 0.0 copy-start.1
  87.7 1.2 copy-done.1
  88.8 41.7 %shard_map.125 = bf16[64,1024]{1,0:T(8,128)(2,1)} custom-call(bf16[256,1024]{1,0:T(8,128)(2,1)} %bitcast.21, bf16[64,1024]{1,0:T(8,128)(2,1)} %get-tuple-element.13.value_ref.patch_ref, f32[64,1]{1,0:T(8,128)} %fusion.9.used_ref, f32[1,1024]{1,0:T(1,128)} %bitcast.22, f32[256,128]{1,0:T(8,128)} %pad_maximum_fusion.cos_ref, ...), custom_call_target="tpu_custom_call" | custom-call | tf_op jit(solution)/shard_map/pallas_call | solution.py:894
  130.6 1.9 %copy.27 = bf16[256,1024]{1,0:T(8,128)(2,1)} copy(bf16[256,1024]{1,0:T(8,128)(2,1)} %get-tuple-element.29) | data formatting | bytes 1048576
  132.4 1.6 %copy.28 = bf16[64,1024]{1,0:T(8,128)(2,1)} copy(bf16[64,1024]{1,0:T(8,128)(2,1)} %shard_map.125) | data formatting | bytes 262144
  (7 shorter events, 0.1 us)
Async XLA Ops:
  0.6 6.7 %copy-start = (bf16[3,1024,256]{2,1,0:T(8,128)(2,1)S(1)}, bf16[3,1024,256]{2,1,0:T(8,128)(2,1)}, u32[]{:S(2)}) copy-start(bf16[3,1024,256]{2,1,0:T(8,128)(2,1)} %param.13) | copy-start | bytes 4718596
  0.6 87.0 %collective-permute-start.1 = (bf16[512,512]{1,0:T(8,128)(2,1)}, bf16[512,512]{1,0:T(8,128)(2,1)}, u32[]{:S(2)}, u32[]{:S(2)}) collective-permute-start(bf16[512,512]{1,0:T(8,128)(2,1)} %o_own_hbm.1), channel_id=1, source_target_pairs={{0,4},{4,0},{8,12},{12,8},{16,20},{20,16},{24,28},{28,24},{1,5},{5... | collective-permute-start | bytes 1572872 | tf_op jit(solution)/shard_map/ppermute | solution.py:953
  0.7 86.9 %collective-permute-start = (bf16[3,512,512]{2,1,0:T(8,128)(2,1)}, bf16[3,512,512]{2,1,0:T(8,128)(2,1)S(1)}, u32[]{:S(2)}, u32[]{:S(2)}) collective-permute-start(bf16[3,512,512]{2,1,0:T(8,128)(2,1)} %w_own_hbm.1), channel_id=1, source_target_pairs={{0,4},{4,0},{8,12},{12,8},{16,20},{20,16},{24,28},{28,24},{1,5},{5... | collective-permute-start | bytes 4718600 | tf_op jit(solution)/shard_map/ppermute | solution.py:952
  87.7 1.2 copy-start.1

commit v5 on v4

--- a/solution.py
+++ b/solution.py
@@ -318,105 +318,6 @@
     return {"tp": index}
 
 
-def relay(value, count, spread, plane_first, call_id):
-    block = value.shape[1:] if spread else value.shape
-
-    def kernel(value_ref, out_ref, land, send_a, recv_a, send_b, recv_b, own_sem):
-        s, t = lax.axis_index("seq"), lax.axis_index("tp")
-        p, c = s // 2, lax.rem(s, 2)
-
-        def plane(index):
-            return {"seq": 2 * index + c}
-
-        if plane_first:
-            a, b, first, second = p, t, plane, tp_peer
-        else:
-            a, b, first, second = t, p, tp_peer, plane
-        others_a = [lax.rem(a + k, count) for k in range(1, count)]
-        others_b = [lax.rem(b + k, count) for k in range(1, count)]
-        greet([first(i) for i in others_a] + [second(i) for i in others_b])
-        hops = []
-        for k in range(1, count):
-            target = lax.rem(a + k, count)
-            hop = pltpu.make_async_remote_copy(
-                src_ref=value_ref.at[target] if spread else value_ref,
-                dst_ref=land.at[k - 1],
-                send_sem=send_a.at[k - 1],
-                recv_sem=recv_a.at[k - 1],
-                device_id=first(target),
-                device_id_type=MESH,
-            )
-            hop.start()
-            hops.append(hop)
-        onward = []
-        for k in range(count):
-            origin = lax.rem(a + count - k, count)
-            if k == 0:
-                here = value_ref.at[a] if spread else value_ref
-            else:
-                hops[k - 1].wait_recv()
-                here = land.at[k - 1]
-            away = pltpu.make_async_remote_copy(
-                src_ref=here,
-                dst_ref=out_ref.at[b],
-                send_sem=send_b.at[k],
-                recv_sem=recv_b.at[b],
-                device_id=second(origin),
-                device_id_type=MESH,
-            )
-            stay = pltpu.make_async_copy(here, out_ref.at[b], own_sem)
-            onward.append((origin, away, stay))
-
-            @pl.when(origin != b)
-            def _():
-                away.start()
-
-            @pl.when(origin == b)
-            def _():
-                stay.start()
-
-        for q in range(count):
-
-            @pl.when(b != q)
-            def _():
-                pltpu.make_async_remote_copy(
-                    src_ref=land.at[0],
-                    dst_ref=out_ref.at[q],
-                    send_sem=send_b.at[q],
-                    recv_sem=recv_b.at[q],
-                    device_id=second(b),
-                    device_id_type=MESH,
-                ).wait_recv()
-
-        for hop in hops:
-            hop.wait_send()
-        for origin, away, stay in onward:
-
-            @pl.when(origin != b)
-            def _():
-                away.wait_send()
-
-            @pl.when(origin == b)
-            def _():
-                stay.wait()
-
-    return pl.pallas_call(
-        kernel,
-        out_shape=jax.ShapeDtypeStruct((count, *block), value.dtype),
-        in_specs=[pl.BlockSpec(memory_space=pltpu.VMEM)],
-        out_specs=pl.BlockSpec(memory_space=pl.ANY),
-        scratch_shapes=[
-            pltpu.VMEM((count - 1, *block), value.dtype),
-            pltpu.SemaphoreType.DMA((count - 1,)),
-            pltpu.SemaphoreType.DMA((count - 1,)),
-            pltpu.SemaphoreType.DMA((count,)),
-            pltpu.SemaphoreType.DMA((count,)),
-            pltpu.SemaphoreType.DMA,
-        ],
-        compiler_params=pltpu.CompilerParams(collective_id=call_id, has_side_effects=True),
-    )(value)
-
-
 def like(shape, dtype=jnp.bfloat16):
     return jax.ShapeDtypeStruct(shape, dtype)
 
@@ -467,15 +368,23 @@
     columns = lift.shape[1]
     total_rows = byte_rows + EDGE
     reach = behind.shape[0]
+    group = 2 * HD
+    panel_count = columns // group
 
     def kernel(
         own_ref, behind_ref, next_ref, proj_ref, states_ref, edge_ref, lo_ref, hi_ref, used_ref,
         lift_hbm, cross_hbm,
-        enc_ref, patch_ref,
-        sends, lands, tail_send, tail_land, blocks, lift_ref, cross_ref, pooled_ref, full_ref,
+        enc_ref, patch_ref, rows_ref,
+        sends, lands, tail_send, tail_land, blocks, lift_ref, cross_ref, pooled_ref, full_ref, panels, z_land,
         load_sems, rs_send, rs_recv, tail_s, tail_r, up_send, down_send, ag_recv,
+        z_send, z_recv, plane_send, plane_recv, stay_sems,
     ):
-        t = lax.axis_index("tp")
+        s, t = lax.axis_index("seq"), lax.axis_index("tp")
+        p, c = s // 2, lax.rem(s, 2)
+
+        def plane(index):
+            return {"seq": 2 * index + c}
+
         loads = [
             pltpu.make_async_copy(lift_hbm, lift_ref, load_sems.at[0]),
             pltpu.make_async_copy(cross_hbm, cross_ref, load_sems.at[1]),
@@ -519,7 +428,10 @@
                 begin = q * share + h * piece
                 sends[q, h] = blend[begin : begin + piece]
         tail_send[...] = blend[byte_rows:]
-        greet([tp_peer(lax.rem(t + k, count)) for k in range(1, count)])
+        greet(
+            [tp_peer(lax.rem(t + k, count)) for k in range(1, count)]
+            + [plane(lax.rem(p + k, count)) for k in range(1, count)]
+        )
         scatter = [[], []]
         for h in range(chunks):
             for k in range(1, count):
@@ -618,7 +530,16 @@
             member.astype(jnp.bfloat16), full_ref[...], preferred_element_type=jnp.float32
         )
         pooled_ref[...] = (totals / lengths).astype(jnp.bfloat16)
-        group = 2 * HD
+
+        def across(k, i):
+            return pltpu.make_async_remote_copy(
+                src_ref=panels.at[i],
+                dst_ref=z_land.at[k - 1, i],
+                send_sem=z_send.at[k - 1, i],
+                recv_sem=z_recv.at[k - 1, i],
+                device_id=tp_peer(lax.rem(t + k, count)),
+                device_id_type=MESH,
+            )
 
         def heads(i, carry):
             cols = pl.ds(pl.multiple_of(i * group, group), group)
@@ -645,10 +566,68 @@
                     jnp.dot(weights, values[:, lanes], preferred_element_type=jnp.float32)
                 )
             patch = lifted + jnp.concatenate(crossed, axis=1)
-            patch_ref[:, cols] = jnp.where(in_use, patch, 0.0).astype(jnp.bfloat16)
+            panel = jnp.where(in_use, patch, 0.0).astype(jnp.bfloat16)
+            patch_ref[:, cols] = panel
+            panels[i] = panel
+            for k in range(1, count):
+                across(k, i).start()
             return carry
 
-        lax.fori_loop(0, columns // group, heads, 0)
+        lax.fori_loop(0, panel_count, heads, 0)
+        onward = []
+        for i in range(panel_count):
+            for k in range(count):
+                origin = lax.rem(t + count - k, count)
+                if k == 0:
+                    here = panels.at[i]
+                else:
+                    across(k, i).wait_recv()
+                    here = z_land.at[k - 1, i]
+                away = pltpu.make_async_remote_copy(
+                    src_ref=here,
+                    dst_ref=rows_ref.at[p, i],
+                    send_sem=plane_send.at[k, i],
+                    recv_sem=plane_recv.at[p, i],
+                    device_id=plane(origin),
+                    device_id_type=MESH,
+                )
+                stay = pltpu.make_async_copy(here, rows_ref.at[p, i], stay_sems.at[i])
+                onward.append((origin, away, stay))
+
+                @pl.when(origin != p)
+                def _():
+                    away.start()
+
+                @pl.when(origin == p)
+                def _():
+                    stay.start()
+
+        for q in range(count):
+
+            @pl.when(p != q)
+            def _():
+                for i in range(panel_count):
+                    pltpu.make_async_remote_copy(
+                        src_ref=panels.at[i],
+                        dst_ref=rows_ref.at[q, i],
+                        send_sem=plane_send.at[q, i],
+                        recv_sem=plane_recv.at[q, i],
+                        device_id=plane(p),
+                        device_id_type=MESH,
+                    ).wait_recv()
+
+        for i in range(panel_count):
+            for k in range(1, count):
+                across(k, i).wait_send()
+        for origin, away, stay in onward:
+
+            @pl.when(origin != p)
+            def _():
+                away.wait_send()
+
+            @pl.when(origin == p)
+            def _():
+                stay.wait()
 
         for h in range(chunks):
             for copy in scatter[h]:
@@ -671,9 +650,13 @@
     dma = pltpu.SemaphoreType.DMA
     return pl.pallas_call(
         kernel,
-        out_shape=[like((byte_rows, width)), like((slots, columns))],
+        out_shape=[
+            like((byte_rows, width)),
+            like((slots, columns)),
+            like((count, panel_count, slots, group)),
+        ],
         in_specs=[vmem] * 9 + [hbm] * 2,
-        out_specs=[vmem, vmem],
+        out_specs=[vmem, vmem, hbm],
         scratch_shapes=[
             pltpu.VMEM((count, chunks, piece, width), jnp.bfloat16),
             pltpu.VMEM((chunks, count - 1, piece, width), jnp.bfloat16),
@@ -684,6 +667,8 @@
             pltpu.VMEM(cross_kv.shape, cross_kv.dtype),
             pltpu.VMEM((slots, width), jnp.bfloat16),
             pltpu.VMEM((total_rows, width), jnp.bfloat16),
+            pltpu.VMEM((panel_count, slots, group), jnp.bfloat16),
+            pltpu.VMEM((count - 1, panel_count, slots, group), jnp.bfloat16),
             dma((2,)),
             dma((chunks, count - 1)),
             dma((chunks, count - 1)),
@@ -692,6 +677,11 @@
             dma((count, chunks)),
             dma((count, chunks)),
             dma((count, chunks)),
+            dma((count - 1, panel_count)),
+            dma((count - 1, panel_count)),
+            dma((count, panel_count)),
+            dma((count, panel_count)),
+            dma((panel_count,)),
         ],
         compiler_params=pltpu.CompilerParams(collective_id=call_id, has_side_effects=True),
     )(projected, behind, edge, proj, byte_states, edge_states, *bounds, used, lift, cross_kv)
@@ -699,7 +689,8 @@
 
 def latent_stage(rows, patches, used, gain, weights, projs, cosine, sine, query_pos, key_pos, call_id):
     count = lax.axis_size("tp")
-    row_total, chip_width = rows.shape
+    pair_count, panel_count, slot_count, group = rows.shape
+    row_total, chip_width = pair_count * slot_count, panel_count * group
     half = chip_width // 2
     slots, columns = patches.shape
     full_width = columns * count
@@ -742,7 +733,9 @@
                 device_id_type=MESH,
             )
 
-        values = rows_ref[...].astype(jnp.float32)
+        values = jnp.concatenate(
+            [rows_ref[:, i].reshape(row_total, group) for i in range(panel_count)], axis=1
+        ).astype(jnp.float32)
         squares = jnp.sum(values * values, axis=1, keepdims=True)
         eye = lax.broadcasted_iota(jnp.int32, (row_total, row_total), 0) == lax.broadcasted_iota(
             jnp.int32, (row_total, row_total), 1
@@ -977,7 +970,7 @@
     lower = jnp.where(in_use, local_starts - anchor, 0)[:, None]
     upper = jnp.where(in_use, patch_end - anchor, 1)[:, None]
     used_rows = in_use.astype(jnp.float32)[:, None]
-    encoded, patches = encode_and_patch(
+    encoded, patches, rows = encode_and_patch(
         projected,
         behind,
         edge,
@@ -1002,8 +995,7 @@
     position, rows_used = slots_of(c)
     other_position, other_used = slots_of(1 - c)
 
-    rows = relay(patches, pairs, False, False, 4).reshape(pairs * slot_total, -1)
-    half = rows.shape[1] // 2
+    half = lat_qkv.shape[1]
     gain = lax.dynamic_slice_in_dim(latent_gain, p * 2 * half, 2 * half, 0).astype(jnp.float32)
     frequency = jnp.power(
         rope_base, -2.0 * jnp.arange(HD // 2, dtype=jnp.float32) / HD

time: 135 us -> 127 us (0.941)
  Pallas kernels: 111 us -> 103 us
    pallas_call x1 -> x0, Pallas kernels: 15.1 us -> none  [relay(): pl.pallas_call(kernel, out_shape=jax.ShapeDtypeStruct((count, *block), va...]
    pallas_call x1, Pallas kernels: 39.8 us -> 48.1 us  [encode_and_patch(): pl.pallas_call(kernel, out_shape=[like((byte_rows, width)), like((slots,...]
  transfers between devices with their start and end apart: 2 -> 2, of which waited for: 0 -> 0; matrix products, arithmetic and copies ran while one was open for 12% -> 13% of each run, Pallas kernels for 51% -> 49%
where the time goes in v5:
time: 127 us; the launch traced here: 126 us
  Pallas kernels  103 us (81%)
  other arithmetic  10.6 us (8%)
  local copies, waits for them, and re-layouts  7.81 us (6%)
  matrix products  2.42 us (2%)
  between operations  2.05 us (2%)
    pallas_call x1, Pallas kernels, encode_and_patch(): pl.pallas_call(kernel, out_shape=[like((byte_rows, width)), like((slots,...  48.1 us
    pallas_call x1, Pallas kernels, latent_stage(): pl.pallas_call(kernel, out_shape=like((slots, columns)), in_specs=[vmem]...  41 us
    pallas_call x1, Pallas kernels, exchange(): pl.pallas_call(kernel, out_shape=out_shapes, in_specs=[pl.BlockSpec(memor...  13.9 us
    unnamed x6, local copies, waits for them, and re-layouts  4.6 us
  transfers between devices with their start and end apart: 2, of which 0 were waited for; matrix products, arithmetic and copies ran while one was open for 13% of the time, Pallas kernels for 49%

profile of v5, /device:TPU:6, one launch (start us, length us, event | category | flops | bytes accessed | tf_op | source)
XLA Modules:
  0.0 126.4 jit_solution(13087187639096244877)
XLA Ops:
  0.6 0.0 copy-start
  0.6 0.1 collective-permute-start.1
  0.7 0.5 collective-permute-start
  1.9 0.7 slice_bitcast_fusion
  2.6 0.6 compare_select_fusion.2
  3.3 0.7 subtract_bitcast_fusion
  4.0 1.2 fusion.1
  5.2 0.6 broadcast_select_fusion.1.refs_2_
  5.8 0.7 convert_element_type.36
  6.5 0.1 copy.21
  6.6 0.1 pad_add_fusion.2
  6.7 0.1 copy.22
  6.8 0.0 copy-done
  6.8 2.4 %fusion.refs_0_.own_ref = bf16[3,256,256]{2,1,0:T(8,128)(2,1)} fusion(bf16[3,1024,256]{2,1,0:T(8,128)(2,1)S(1)} %copy-done, bf16[256,1024]{1,0:T(8,128)(2,1)} %states_ref.1, f32[1024]{0:T(1024)S(1)} %convert_element_type.36, f32[256]{0:T(256)S(1)} %add_rsqrt_fusion), kind=kOutput, calls=%fused_computation.3 | convolution fusion | flops 403898368 | bytes 2495488 | tf_op jit(solution)/shard_map/bd,idc->ibc/dot_general | solution.py:949
  9.2 13.9 %shard_map.122 = (bf16[2,2,256,256]{3,2,1,0:T(8,128)(2,1)}, bf16[3,16,256]{2,1,0:T(8,128)(2,1)}, bf16[16,1024]{1,0:T(8,128)(2,1)}, s32[7,8,128]{2,1,0:T(8,128)}) custom-call(bf16[3,256,256]{2,1,0:T(8,128)(2,1)} %fusion.refs_0_.own_ref, bf16[256,1024]{1,0:T(8,128)(2,1)} %states_ref.1, s32[8,128]{1,0:T(8,128)} %broadcast_select_fusion.1.refs_2_), custom_call_target="tpu_custom_call" | custom-call | tf_op jit(solution)/shard_map/pallas_call | solution.py:292
  23.0 1.3 slice.16
  24.3 1.0 fusion.11
  25.3 0.1 select_reduce_fusion.1
  25.4 0.1 select_reduce_fusion
  25.5 0.2 select_reduce_fusion.4
  25.7 0.1 fusion.12
  25.8 0.1 select_n.102
  25.9 0.1 convert_element_type.42
  26.0 0.1 select_n.106
  26.1 0.8 add.125.qpos_ref
  27.5 0.6 fusion.9.used_ref
  28.1 0.6 subtract_select_fusion
  28.7 48.1 %shard_map.123 = (bf16[256,1024]{1,0:T(8,128)(2,1)}, bf16[64,1024]{1,0:T(8,128)(2,1)}, bf16[4,4,64,256]{3,2,1,0:T(8,128)(2,1)}) custom-call(bf16[3,256,256]{2,1,0:T(8,128)(2,1)} %fusion.refs_0_.own_ref, bf16[2,2,256,256]{3,2,1,0:T(8,128)(2,1)} %get-tuple-element.9.behind_ref, bf16[3,16,256]{2,1,0:T(8,128)(2,1)} %get-tuple-element.10.next_ref, ...), custom_call_target="tpu_custom_call" | custom-call | tf_op jit(solution)/shard_map/pallas_call | solution.py:651
  76.9 0.6 pad_add_fusion.1
  77.5 1.3 %dynamic-slice_convert_fusion = f32[1024]{0:T(1024)} fusion(bf16[4096]{0:T(1024)(128)(2,1)} %param.19, s32[]{:T(128)S(6)} %select_n.95), kind=kLoop, calls=%fused_computation.40 | loop fusion | flops 1024 | bytes 6148 | tf_op jit(solution)/shard_map/broadcast_in_dim | solution.py:1016
  78.7 0.5 fusion.8
  79.3 0.8 pad_maximum_fusion.cos_ref
  80.0 0.8 pad_maximum_fusion.1.sin_ref
  80.8 0.0 collective-permute-done.1.o_other_hbm
  80.8 0.0 collective-permute-done.w_other_hbm
  80.8 0.0 copy-start.1
  80.8 1.2 copy-done.1
  82.0 41.0 %shard_map.124 = bf16[64,1024]{1,0:T(8,128)(2,1)} custom-call(bf16[4,4,64,256]{3,2,1,0:T(8,128)(2,1)} %get-tuple-element.14.rows_ref, bf16[64,1024]{1,0:T(8,128)(2,1)} %get-tuple-element.15.patch_ref, f32[64,1]{1,0:T(8,128)} %fusion.9.used_ref, f32[1,1024]{1,0:T(1,128)} %bitcast.20, f32[256,128]{1,0:T(8,128)} %pad_maximum_fusion.cos_ref, ...), custom_call_target="tpu_custom_call" | custom-call | tf_op jit(solution)/shard_map/pallas_call | solution.py:887
  123.0 1.9 %copy.27 = bf16[256,1024]{1,0:T(8,128)(2,1)} copy(bf16[256,1024]{1,0:T(8,128)(2,1)} %get-tuple-element.31) | data formatting | bytes 1048576
  124.8 1.6 %copy.28 = bf16[64,1024]{1,0:T(8,128)(2,1)} copy(bf16[64,1024]{1,0:T(8,128)(2,1)} %shard_map.124) | data formatting | bytes 262144
  (7 shorter events, 0.0 us)
Async XLA Ops:
  0.6 6.1 %copy-start = (bf16[3,1024,256]{2,1,0:T(8,128)(2,1)S(1)}, bf16[3,1024,256]{2,1,0:T(8,128)(2,1)}, u32[]{:S(2)}) copy-start(bf16[3,1024,256]{2,1,0:T(8,128)(2,1)} %param.13) | copy-start | bytes 4718596
  0.6 80.2 %collective-permute-start.1 = (bf16[512,512]{1,0:T(8,128)(2,1)}, bf16[512,512]{1,0:T(8,128)(2,1)}, u32[]{:S(2)}, u32[]{:S(2)}) collective-permute-start(bf16[512,512]{1,0:T(8,128)(2,1)} %o_own_hbm.1), channel_id=1, source_target_pairs={{0,4},{4,0},{8,12},{12,8},{16,20},{20,16},{24,28},{28,24},{1,5},{5... | collective-permute-start | bytes 1572872 | tf_op jit(solution)/shard_map/ppermute | solution.py:946
  0.7 80.1 %collective-permute-start = (bf16[3,512,512]{2,1,0:T(8,128)(2,1)}, bf16[3,512,512]{2,1,0:T(8,128)(2,1)S(1)}, u32[]{:S(2)}, u32[]{:S(2)}) collective-permute-start(bf16[3,512,512]{2,1,0:T(8,128)(2,1)} %w_own_hbm.1), channel_id=1, source_target_pairs={{0,4},{4,0},{8,12},{12,8},{16,20},{20,16},{24,28},{28,24},{1,5},{5... | collective-permute-start | bytes 4718600 | tf_op jit(solution)/shard_map/ppermute | solution.py:945
  80.8 1.2 copy-start.1
